TPU v7x, 128 devices: a whole 4x4x4 slice. The times are simulated.
128 devices in a mesh: tgt: 4 (over x), inner: 32 (over z, y, core).
Axes of the slice: x: 4, y: 4, z: 4, core: 2. Of those that a mesh axis runs over, the one named last changes fastest.
Arguments:
- near_tiles: bfloat16 [512, 1024, 1024], P(('tgt', 'inner')), may hold values from -0.1875 to 0.1875
- near_target: int32 [512], P(('tgt', 'inner')), may hold values from 0 to 7
- near_right: int32 [512], P(('tgt', 'inner')), may hold values from 0 to 31
- near_count: int32 [128], P(('tgt', 'inner')), may hold values from 1 to 4, as said below
- low_u: bfloat16 [4096, 64, 1024], P(('tgt', 'inner')), may hold values from -0.75 to 0.75
- low_v: bfloat16 [4096, 64, 1024], P(('tgt', 'inner')), may hold values from -0.1875 to 0.1875
- low_target: int32 [4096], P(('tgt', 'inner')), may hold values from 0 to 7, as said below
- low_right: int32 [4096], P(('tgt', 'inner')), may hold values from 0 to 31
- right_u: bfloat16 [1024, 64, 1024], P(('tgt', 'inner')), may hold values from -6 to 6
- right_v: bfloat16 [1024, 64, 1024], P(('tgt', 'inner')), may hold values from -0.125 to 0.125
- probe_seed: int32 [32], P('tgt'), may hold values from 1 to 29999
Outputs:
- basis_out: float32 [32, 64, 1024], P('tgt', None, 'inner')
- image_out: float32 [32, 64, 1024], P('tgt', None, 'inner')
Inputs may be any that keep to these rules, and one draw needn't show every extreme that they name: `near_count`: some device holds 4 live slots. `low_target`: the 32 low-rank pairs of each device name every target tile of its group.
All inputs are finite; a program needn't handle non-finite values.
Results may differ from a plain program's by a relative error of at most 0.004.
Values may be sent and summed in bfloat16 or wider, within the bound.
No kernel may reach another device: no remote copies, remote signals or barrier semaphores. Data moves between devices by JAX's collectives and lax.ppermute only.
A program may use at most 128 MiB of HBM per device.

v0:
```python
import jax
import jax.numpy as jnp
from jax import lax
from jax.experimental import pallas as pl
from jax.experimental.pallas import tpu as pltpu
from jax.sharding import PartitionSpec as P


B = 1024
R = 64
MOD = 65521
N_LOW = 32
N_NEAR = 4
N_PAIR = N_LOW + N_NEAR
HALF = N_PAIR // 2
F32 = jnp.float32
BF16 = jnp.bfloat16


M_T = N_PAIR
M_COUNT = 2 * N_PAIR
M_CORE = M_COUNT + 1
M_Z = M_COUNT + 2
M_Y = M_COUNT + 3
M_S = M_COUNT + 4

SMEM = pl.BlockSpec(memory_space=pltpu.MemorySpace.SMEM)
VM = pl.BlockSpec(memory_space=pltpu.MemorySpace.VMEM)
ANY = pl.BlockSpec(memory_space=pltpu.MemorySpace.HBM)
PARAMS = pltpu.CompilerParams(vmem_limit_bytes=32 * 1024 * 1024)
SMALL = pltpu.CompilerParams(vmem_limit_bytes=12 * 1024 * 1024)


def in_hbm(*xs):
    return tuple(pltpu.with_memory_space_constraint(x, pltpu.MemorySpace.HBM) for x in xs)


def dot_nt(a, b):
    return lax.dot_general(a, b, (((1,), (1,)), ((), ())), preferred_element_type=F32)


def dot_nn(a, b):
    return lax.dot_general(a, b, (((1,), (0,)), ((), ())), preferred_element_type=F32)


def split2(x):
    hi = x.astype(BF16)
    return hi, (x - hi.astype(F32)).astype(BF16)


def zeta_kernel(req, v_ref, o0, o1, o2, o3, base, probe, tab):
    c = lax.broadcasted_iota(jnp.int32, (R, B), 0)
    i = lax.broadcasted_iota(jnp.int32, (R, B), 1)
    f = i * i * 7 + i * c * 131 + c * c * 17 + i * 7919 + c * 104729
    q = (f.astype(F32) * (1.0 / MOD)).astype(jnp.int32)
    f = f - q * MOD
    f = jnp.where(f < 0, f + MOD, f)
    f = jnp.where(f >= MOD, f - MOD, f)
    base[...] = f.astype(F32)
    v = v_ref[...].reshape(8 * R, B)
    left = lax.broadcasted_iota(jnp.int32, (4 * R, 128), 1) < R

    def batch(b, carry):
        row = b // 2
        for u in range(4):
            seed = req[row, 2 * N_PAIR + (b % 2) * 4 + u]
            shift = lax.rem(seed * 9973, MOD).astype(F32)
            code = base[...] + shift
            code = jnp.where(code >= MOD, code - MOD, code)
            probe[u * R : (u + 1) * R] = ((code - 32760.0) * (1.0 / 32768.0)).astype(BF16)
        res = dot_nt(probe[...], v)
        for ip in range(4):
            blk = res[:, ip * 128 : (ip + 1) * 128]
            rolled = pltpu.roll(blk, R, 1)
            even = jnp.where(left, blk, rolled)
            odd = jnp.where(left, rolled, blk)
            for u in range(4):
                tab[b * 4 + u, 2 * ip] = even[u * R : (u + 1) * R]
                tab[b * 4 + u, 2 * ip + 1] = odd[u * R : (u + 1) * R]
        return carry

    lax.fori_loop(0, 8, batch, 0)
    lm = lax.broadcasted_iota(jnp.int32, (R, 128), 1) < R

    def slot(p, carry):
        for q, out in enumerate((o0, o1, o2, o3)):
            ra = req[q, p] & 7
            ta = req[q, N_PAIR + p]
            rb = req[q, HALF + p] & 7
            tb = req[q, N_PAIR + HALF + p]
            out[p] = jnp.where(lm, tab[q * 8 + ta, ra], tab[q * 8 + tb, rb]).astype(BF16)
        return carry

    lax.fori_loop(0, HALF, slot, 0)


def zeta_home(req, v_own):
    out = jax.ShapeDtypeStruct((HALF, R, 128), BF16)
    return pl.pallas_call(
        zeta_kernel,
        out_shape=(out,) * 4,
        in_specs=[SMEM, VM],
        out_specs=(VM,) * 4,
        scratch_shapes=[
            pltpu.VMEM((R, B), F32),
            pltpu.VMEM((4 * R, B), BF16),
            pltpu.VMEM((32, 8, R, 128), F32),
        ],
        compiler_params=PARAMS,
        name="zeta_home",
    )(req, v_own)


PLUS_TILES = 2


def start_tile(r, own, dst, sem):
    for cond, ref, shift in own(r):

        @pl.when(cond)
        def _():
            pltpu.make_async_copy(ref.at[(r & 7) - shift], dst, sem).start()


def build_plan(meta, plan):
    def per_target(t, slot):
        def per_pair(j, at):
            hit = meta[M_T + j] == t

            @pl.when(hit)
            def _():
                plan[at] = j + 256

            return at + hit.astype(jnp.int32)

        end = lax.fori_loop(0, N_LOW, per_pair, slot)
        full = (end + 3) // 4 * 4

        @pl.when(end > slot)
        def _():
            plan[64 + slot // 4] = t

            def more(c, carry):
                plan[64 + c] = t
                return carry

            lax.fori_loop(slot // 4, full // 4, more, 0)

            def pad(i, carry):
                plan[i] = plan[end - 1] & 255
                return carry

            lax.fori_loop(end, full, pad, 0)

        return full

    plan[127] = lax.fori_loop(0, 8, per_target, 0)


def pairs_body(meta, mine, own, zbuf, lv, lu, nt, mix, lt, acc, lst, lvb, lub, ub, nb, unb, sems, nsems):
    def low(j, n):
        r = meta[j]
        hit = mine(r >> 3)

        @pl.when(hit)
        def _():
            lst[n] = j
            pltpu.make_async_copy(lv.at[j], lvb.at[n], sems.at[0, n]).start()
            start_tile(r, own, ub.at[n], sems.at[1, n])
            pltpu.make_async_copy(lu.at[j], lub.at[n], sems.at[2, n]).start()

        return n + hit.astype(jnp.int32)

    n = lax.fori_loop(0, N_LOW, low, 0)

    def near(s, m):
        r = meta[N_LOW + s]
        hit = mine(r >> 3) & (s < meta[M_COUNT])

        @pl.when(hit)
        def _():
            lst[N_LOW + m] = s
            pltpu.make_async_copy(nt.at[s], nb.at[m], nsems.at[0, m]).start()
            start_tile(r, own, unb.at[m], nsems.at[1, m])

        return m + hit.astype(jnp.int32)

    nn = lax.fori_loop(0, N_NEAR, near, 0)

    def zeta(j):
        second = j >= HALF
        blk = zbuf[meta[j] >> 3, jnp.where(second, j - HALF, j)].astype(F32)
        return jnp.where(second, pltpu.roll(blk, R, 1), blk)[:, :R].astype(BF16)

    def group(g, carry):
        for i in range(4):
            pos = g * 4 + i

            @pl.when(pos < n)
            def _():
                pltpu.make_async_copy(lv.at[0], lvb.at[pos], sems.at[0, pos]).wait()
                pltpu.make_async_copy(lv.at[0], ub.at[pos], sems.at[1, pos]).wait()
                pltpu.make_async_copy(lu.at[0], lub.at[pos], sems.at[2, pos]).wait()

        for i in range(4):
            valid = (g * 4 + i < n).astype(F32)
            pos = jnp.minimum(g * 4 + i, n - 1)
            j = lst[pos]
            mt = dot_nt(ub[pos], lvb[pos]).astype(BF16)
            mix[j] = mt
            hi, lo = split2(dot_nn(zeta(j), mt) * valid)
            res = dot_nn(jnp.concatenate([hi, lo], axis=0), lub[pos])
            acc[meta[M_T + j]] += res[:R] + res[R:]
        return carry

    lax.fori_loop(0, (n + 3) // 4, group, 0)

    def tile(m, carry):
        s = lst[N_LOW + m]
        pltpu.make_async_copy(nt.at[0], nb.at[m], nsems.at[0, m]).wait()
        pltpu.make_async_copy(lv.at[0], unb.at[m], nsems.at[1, m]).wait()
        left = dot_nt(unb[m], nb[m]).astype(BF16)
        lt[s] = left
        acc[meta[M_T + N_LOW + s]] += dot_nn(zeta(N_LOW + s), left)
        return carry

    lax.fori_loop(0, nn, tile, 0)


def pairs_a_kernel(meta, u0, u1, u3, z0, z1, z3, lv, lu, nt, acc, mix, lt, plan, zbuf, *scratch):
    def own(r):
        rel = r >> 3
        return ((rel == 0, u0, 0), (rel == 1, u1, 0), (rel == 3, u3, 0))

    acc[...] = jnp.zeros_like(acc)
    for n, ref in ((0, z0), (1, z1), (3, z3)):
        zbuf[n] = ref[...]
    pairs_body(meta, lambda rel: rel != 2, own, zbuf, lv, lu, nt, mix, lt, acc, *scratch)
    build_plan(meta, plan)


def pairs_b_kernel(meta, u2a, u2b, z2, acc_in, lv, lu, nt, keep, send, mix, lt, zbuf, acc, *scratch):
    def own(r):
        first = (r & 7) < PLUS_TILES
        return ((first, u2a, 0), (jnp.logical_not(first), u2b, PLUS_TILES))

    acc[...] = acc_in[...]
    zbuf[2] = z2[...]
    pairs_body(meta, lambda rel: rel == 2, own, zbuf, lv, lu, nt, mix, lt, acc, *scratch)
    core = meta[M_CORE]
    keep[...] = acc[pl.ds(core * 4, 4)]
    send[...] = acc[pl.ds(4 - core * 4, 4)]


ACC = jax.ShapeDtypeStruct((8, R, B), F32)
MIX = jax.ShapeDtypeStruct((N_LOW, R, R), BF16)
LEFT = jax.ShapeDtypeStruct((N_NEAR, R, B), BF16)
QUAD = jax.ShapeDtypeStruct((4, R, B), F32)
PAIR_SCRATCH = [
    pltpu.SMEM((N_PAIR,), jnp.int32),
    pltpu.VMEM((N_LOW, R, B), BF16),
    pltpu.VMEM((N_LOW, R, B), BF16),
    pltpu.VMEM((N_LOW, R, B), BF16),
    pltpu.VMEM((N_NEAR, B, B), BF16),
    pltpu.VMEM((N_NEAR, R, B), BF16),
    pltpu.SemaphoreType.DMA((3, N_LOW)),
    pltpu.SemaphoreType.DMA((2, N_NEAR)),
]
ZBUF = pltpu.VMEM((4, HALF, R, 128), BF16)


def pairs_a(meta, us, zs, low_v, low_u, near):
    return pl.pallas_call(
        pairs_a_kernel,
        out_shape=(ACC, MIX, LEFT, jax.ShapeDtypeStruct((128,), jnp.int32)),
        in_specs=[SMEM] + [ANY] * 3 + [VM] * 3 + [ANY] * 3,
        out_specs=(VM, VM, VM, SMEM),
        scratch_shapes=[ZBUF] + PAIR_SCRATCH,
        compiler_params=PARAMS,
        name="pairs_a",
    )(meta, *in_hbm(*us), *zs, *in_hbm(low_v, low_u, near))


def pairs_b(meta, us, z2, acc, low_v, low_u, near):
    return pl.pallas_call(
        pairs_b_kernel,
        out_shape=(QUAD, QUAD, MIX, LEFT),
        in_specs=[SMEM] + [ANY] * 2 + [VM, VM] + [ANY] * 3,
        out_specs=(VM,) * 4,
        scratch_shapes=[ZBUF, pltpu.VMEM((8, R, B), F32)] + PAIR_SCRATCH,
        compiler_params=PARAMS,
        name="pairs_b",
    )(meta, *in_hbm(*us), z2, acc, *in_hbm(low_v, low_u, near))


SLOTS = 56


def image_kernel(
    meta, plan, s0, s1, s2, s3, r0, r1, r2, r3, v0, v1, v2a, v2b, v3, lu, mixa, mixb, lta, ltb,
    keep, send, sall, lub, vb, nvb, acc, sems, nsems
):
    def own(r):
        rel = r >> 3
        low = (r & 7) < 4
        return (
            (rel == 0, v0, 0),
            (rel == 1, v1, 0),
            ((rel == 2) & low, v2a, 0),
            ((rel == 2) & jnp.logical_not(low), v2b, 4),
            (rel == 3, v3, 0),
        )

    count = plan[127]

    def load(i, carry):
        j = plan[i] & 255
        pltpu.make_async_copy(lu.at[j], lub.at[i], sems.at[0, i]).start()
        start_tile(meta[j], own, vb.at[i], sems.at[1, i])
        return carry

    lax.fori_loop(0, count, load, 0)
    live = meta[M_COUNT]

    def nload(s, carry):
        start_tile(meta[N_LOW + s], own, nvb.at[s], nsems.at[s])
        return carry

    lax.fori_loop(0, live, nload, 0)
    acc[...] = jnp.zeros_like(acc)
    core = meta[M_CORE]
    z = meta[M_Z]
    for n, ref in enumerate((s0, s1, s2, s3)):
        sall[core * 4 + ((z + n) & 3)] = ref[...]
    for n, ref in enumerate((r0, r1, r2, r3)):
        sall[(1 - core) * 4 + ((z + n) & 3)] = ref[...]

    def chunk(m, carry):
        at = m * 4
        for i in range(4):
            pltpu.make_async_copy(lu.at[0], lub.at[at + i], sems.at[0, at + i]).wait()
        t = plan[64 + m]
        q = dot_nt(lub[pl.ds(at, 4)].reshape(4 * R, B), sall[t])
        parts = []
        for i in range(4):
            e = plan[at + i]
            j = e & 255
            mt = jnp.where((meta[j] >> 3) == 2, mixb[j], mixa[j])
            hi, lo = split2(q[i * R : (i + 1) * R])
            both = dot_nn(mt, jnp.concatenate([hi, lo], axis=1))
            parts.append((both[:, :R] + both[:, R:]) * (e >> 8).astype(F32))
        p = jnp.concatenate(parts, axis=0).T
        hi, lo = split2(p)
        for i in range(4):
            pltpu.make_async_copy(lu.at[0], vb.at[at + i], sems.at[1, at + i]).wait()
        res = dot_nn(jnp.concatenate([hi, lo], axis=0), vb[pl.ds(at, 4)].reshape(4 * R, B))
        acc[t] += res[:R] + res[R:]
        return carry

    lax.fori_loop(0, count // 4, chunk, 0)

    def near(s, carry):
        t = meta[M_T + N_LOW + s]
        left = jnp.where((meta[N_LOW + s] >> 3) == 2, ltb[s], lta[s])
        hi, lo = split2(dot_nt(sall[t], left))
        pltpu.make_async_copy(lu.at[0], nvb.at[s], nsems.at[s]).wait()
        res = dot_nn(jnp.concatenate([hi, lo], axis=0), nvb[s])
        acc[t] += res[:R] + res[R:]
        return carry

    lax.fori_loop(0, live, near, 0)
    flip = acc[...].reshape(8 * R, B).T.reshape(16, 2, 32, 8 * R)
    first = core == 0
    keep[...] = jnp.where(first, flip[:, 0], flip[:, 1])
    send[...] = jnp.where(first, flip[:, 1], flip[:, 0])


def image_part(meta, plan, tiles, vs, low_u, mixes, lefts):
    half = jax.ShapeDtypeStruct((16, 32, 8 * R), F32)
    return pl.pallas_call(
        image_kernel,
        out_shape=(half, half, jax.ShapeDtypeStruct((8, R, B), BF16)),
        in_specs=[SMEM, SMEM] + [VM] * 8 + [ANY] * 6 + [VM] * 4,
        out_specs=(VM,) * 3,
        scratch_shapes=[
            pltpu.VMEM((SLOTS, R, B), BF16),
            pltpu.VMEM((SLOTS, R, B), BF16),
            pltpu.VMEM((N_NEAR, R, B), BF16),
            pltpu.VMEM((8, R, B), F32),
            pltpu.SemaphoreType.DMA((2, SLOTS)),
            pltpu.SemaphoreType.DMA((N_NEAR,)),
        ],
        compiler_params=PARAMS,
        name="image_part",
    )(meta, plan, *tiles, *in_hbm(*vs, low_u), *mixes, *lefts)


def dot_exact(a, b):
    return lax.dot_general(
        a, b, (((1,), (1,)), ((), ())), precision=lax.Precision.HIGHEST, preferred_element_type=F32
    )


def eliminate(m, ks):
    for k in ks:
        r0 = k // 8 * 8
        block = m[:, r0:, :]
        piv = m[:, k : k + 1, :]
        scaled = piv * (1.0 / piv[:, :, k : k + 1])
        fac = block[:, :, k : k + 1]
        if r0 + 8 > k:
            rows = lax.broadcasted_iota(jnp.int32, fac.shape, 1) + r0
            fac = jnp.where(rows > k, fac, 0.0)
        m[:, r0:, :] = block - fac * scaled


def factor_0_kernel(s_ref, m):
    lane = lax.broadcasted_iota(jnp.int32, (R, 2 * R), 1)
    row = lax.broadcasted_iota(jnp.int32, (R, 2 * R), 0)
    eye = (lane == row + R).astype(F32)
    for t in range(8):
        s = s_ref[t]
        g = dot_nt(s, s)
        m[t] = jnp.where(lane < R, jnp.concatenate([g, g], axis=1), eye)
    eliminate(m, range(CUT0))


def factor_1_kernel(m_in, m):
    m[...] = m_in[...]
    eliminate(m, range(CUT0, CUT1))


def factor_2_kernel(meta, s_ref, m_in, basis, inv, m):
    m[...] = m_in[...]
    eliminate(m, range(CUT1, R))
    lane = lax.broadcasted_iota(jnp.int32, (R, 2 * R), 1)
    row = lax.broadcasted_iota(jnp.int32, (R, 2 * R), 0)
    pick_row = lax.broadcasted_iota(jnp.int32, (32, B), 0) + meta[M_S] * 32
    pick = (lax.broadcasted_iota(jnp.int32, (32, B), 1) == pick_row).astype(BF16)
    for t in range(8):
        a = m[t]
        diag = jnp.sum(jnp.where(lane == row, a, 0.0), axis=1, keepdims=True)
        li = a[:, R:] * lax.rsqrt(diag)
        inv[t] = li
        basis[t] = 32.0 * dot_exact(dot_nt(pick, s_ref[t]), li)


CUT0 = 6
CUT1 = 36
STATE = jax.ShapeDtypeStruct((8, R, 2 * R), F32)


def factor(meta, s):
    m = pl.pallas_call(
        factor_0_kernel, out_shape=STATE, in_specs=[VM], out_specs=VM, compiler_params=SMALL, name="factor_0"
    )(s)
    m = pl.pallas_call(
        factor_1_kernel, out_shape=STATE, in_specs=[VM], out_specs=VM, compiler_params=SMALL, name="factor_1"
    )(m)
    return pl.pallas_call(
        factor_2_kernel,
        out_shape=(jax.ShapeDtypeStruct((8, 32, R), F32), jax.ShapeDtypeStruct((8, R, R), F32)),
        in_specs=[SMEM, VM, VM],
        out_specs=(VM, VM),
        scratch_shapes=[pltpu.VMEM((8, R, 2 * R), F32)],
        compiler_params=SMALL,
        name="factor_2",
    )(meta, s, m)


def first_sum(meta, a, b):
    part = (a.shape[0] // 4,) + a.shape[1:]
    n = part[0]

    def body(meta, a, b, own, p1, p2, p3):
        z = meta[M_Z]
        for k, out in enumerate((own, p1, p2, p3)):
            at = pl.ds(((z + k) & 3) * n, n)
            out[...] = (a[at] + b[at]).astype(out.dtype)

    outs = pl.pallas_call(
        body,
        out_shape=(jax.ShapeDtypeStruct(part, F32),) + (jax.ShapeDtypeStruct(part, BF16),) * 3,
        in_specs=[SMEM, VM, VM],
        out_specs=(VM,) * 4,
        compiler_params=SMALL,
        name="first_sum",
    )(meta, a, b)
    return outs


def add4(a, b, c, d, dtype):
    def body(a, b, c, d, out):
        out[...] = (a[...].astype(F32) + b[...].astype(F32) + c[...].astype(F32) + d[...].astype(F32)).astype(dtype)

    return pl.pallas_call(
        body,
        out_shape=jax.ShapeDtypeStruct(a.shape, dtype),
        in_specs=[VM] * 4,
        out_specs=VM,
        compiler_params=SMALL,
        name="add4",
    )(a, b, c, d)


def second_sum(meta, a, b, c, d):
    shape = a.shape[1:]

    def body(meta, a, b, c, d, own, p1, p2, p3):
        y = meta[M_Y]
        for k, out in enumerate((own, p1, p2, p3)):
            at = (y + k) & 3
            out[...] = a[at] + b[at].astype(F32) + c[at].astype(F32) + d[at].astype(F32)

    return pl.pallas_call(
        body,
        out_shape=(jax.ShapeDtypeStruct(shape, F32),) * 4,
        in_specs=[SMEM] + [VM] * 4,
        out_specs=(VM,) * 4,
        compiler_params=SMALL,
        name="second_sum",
    )(meta, a, b, c, d)


def finish(inv, a, b, c, d):
    def body(inv, a, b, c, d, out):
        total = a[...] + b[...] + c[...] + d[...]
        for t in range(8):
            out[t] = dot_exact(total[:, t * R : (t + 1) * R], inv[t])

    return pl.pallas_call(
        body,
        out_shape=jax.ShapeDtypeStruct((8, 32, R), F32),
        in_specs=[VM] * 5,
        out_specs=VM,
        compiler_params=SMALL,
        name="finish",
    )(inv, a, b, c, d)


def along_x(x, step):
    return lax.ppermute(x, "tgt", [(i, (i + step) % 4) for i in range(4)])


def along_inner(x, dz=0, dy=0, dc=0):
    pairs = []
    for z in range(4):
        for y in range(4):
            for c in range(2):
                to = (((z + dz) % 4) * 4 + (y + dy) % 4) * 2 + (c ^ dc)
                pairs.append(((z * 4 + y) * 2 + c, to))
    return lax.ppermute(x, "inner", pairs)


def after(x, *others):
    return lax.optimization_barrier((x,) + others)[0]


def steps(
    near_tiles, near_target, near_right, near_count, low_u, low_v, low_target, low_right, right_u, right_v, probe_seed
):
    g = lax.axis_index("tgt")
    s = lax.axis_index("inner")
    rights = jnp.concatenate([low_right, near_right])
    targets = jnp.concatenate([low_target, near_target])
    req = jnp.concatenate([rights, targets, probe_seed, jnp.zeros((128 - 2 * N_PAIR - 8,), jnp.int32)])[None]
    place = jnp.stack([near_count[0], s & 1, s >> 3, (s >> 1) & 3, s]).astype(jnp.int32)
    meta = jnp.concatenate(
        [(rights - 8 * g) & 31, targets, place, jnp.zeros((128 - 2 * N_PAIR - 5,), jnp.int32)]
    )

    u3 = along_x(right_u, 1)
    u1 = along_x(right_u, 3)
    reqs = jnp.concatenate([req, along_x(req, 3), along_x(req, 2), along_x(req, 1)])
    o0, o1, o2, o3 = zeta_home(after(reqs, meta), right_v)
    z1 = along_x(o3, 3)
    z3 = along_x(o1, 1)
    z2 = along_x(o2, 2)
    u2a = along_x(u3[:PLUS_TILES], 1)
    u2b = along_x(u1[PLUS_TILES:], 3)
    v3 = along_x(right_v, 1)
    v1 = along_x(right_v, 3)

    acc, mixa, lta, plan = pairs_a(meta, (right_u, u1, u3), (o0, z1, z3), low_v, low_u, near_tiles)
    keep, send, mixb, ltb = pairs_b(meta, (u2a, u2b), z2, acc, low_v, low_u, near_tiles)

    other = along_inner(send, dc=1)
    own, p1, p2, p3 = first_sum(meta, keep, other)
    col = add4(
        own[0], along_inner(p1[0], dz=1), along_inner(p2[0], dz=2), along_inner(p3[0], dz=3), BF16
    )
    v2a = along_x(v3[:4], 1)
    v2b = along_x(v1[4:], 3)
    tile = add4(col, along_inner(col, dy=1), along_inner(col, dy=2), along_inner(col, dy=3), BF16)
    mine = (tile, along_inner(tile, dz=3), along_inner(tile, dz=2), along_inner(tile, dz=1))
    theirs = tuple(along_inner(x, dc=1) for x in mine)

    ikeep, isend, sall = image_part(
        meta, plan, mine + theirs, (right_v, v1, v2a, v2b, v3), low_u, (mixa, mixb), (lta, ltb)
    )
    basis, inv = factor(meta, sall)

    iother = along_inner(isend, dc=1)
    own, p1, p2, p3 = first_sum(meta, ikeep, iother)
    own, p1, p2, p3 = second_sum(
        meta, own, along_inner(p1, dz=1), along_inner(p2, dz=2), along_inner(p3, dz=3)
    )
    image = finish(inv, own, along_inner(p1, dy=1), along_inner(p2, dy=2), along_inner(p3, dy=3))
    return (jnp.swapaxes(basis, 1, 2), jnp.swapaxes(image, 1, 2))


def solution(mesh):
    dev = P(("tgt", "inner"))
    return jax.shard_map(
        steps,
        mesh=mesh,
        in_specs=(dev,) * 10 + (P("tgt"),),
        out_specs=(P("tgt", None, "inner"), P("tgt", None, "inner")),
        check_vma=False,
    )
```

profile of v0, /device:TPU:0, one launch (start us, length us, event | category | flops | bytes accessed | tf_op | source)
XLA Modules:
  0.0 199.4 jit_solution(17298778400390037267)
XLA Ops:
  0.6 2.9 %collective-permute-start = (bf16[8,64,1024]{2,1,0:T(8,128)(2,1)}, bf16[8,64,1024]{2,1,0:T(8,128)(2,1)S(1)}, u32[]{:S(2)}, u32[]{:S(2)}) collective-permute-start(bf16[8,64,1024]{2,1,0:T(8,128)(2,1)} %u0.1), channel_id=1, source_target_pairs={{0,96},{32,0},{64,32},{96,64},{1,97},{33,1},{65,33},{97,65},{2,98}... | collective-permute-start | bytes 3145736 | tf_op jit(solution)/shard_map/ppermute | solution.py:542
  3.6 22.7 %collective-permute-done.u1 = bf16[8,64,1024]{2,1,0:T(8,128)(2,1)S(1)} collective-permute-done((bf16[8,64,1024]{2,1,0:T(8,128)(2,1)}, bf16[8,64,1024]{2,1,0:T(8,128)(2,1)S(1)}, u32[]{:S(2)}, u32[]{:S(2)}) %collective-permute-start) | collective-permute-done | bytes 1048608 | tf_op jit(solution)/shard_map/ppermute | solution.py:542
  27.3 3.6 %collective-permute-start.8 = (bf16[6,64,1024]{2,1,0:T(8,128)(2,1)}, bf16[6,64,1024]{2,1,0:T(8,128)(2,1)S(1)}, u32[]{:S(2)}, u32[]{:S(2)}) collective-permute-start(bf16[6,64,1024]{2,1,0:T(8,128)(2,1)} %slice.17), channel_id=1, source_target_pairs={{0,96},{32,0},{64,32},{96,64},{1,97},{33,1},{65,33},{97,65},{2,98}... | collective-permute-start | bytes 2359304 | tf_op jit(solution)/shard_map/ppermute | solution.py:542
  35.9 11.3 %collective-permute-done.2 = s32[1,128]{1,0:T(1,128)S(1)} collective-permute-done((s32[1,128]{1,0:T(1,128)S(1)}, s32[1,128]{1,0:T(1,128)S(1)}, u32[]{:S(2)}, u32[]{:S(2)}) %collective-permute-start.2) | collective-permute-done | bytes 544 | tf_op jit(solution)/shard_map/ppermute | solution.py:542
  47.2 7.1 %zeta_home.1 = (bf16[18,64,128]{2,1,0:T(8,128)(2,1)S(1)}, bf16[18,64,128]{2,1,0:T(8,128)(2,1)S(1)}, bf16[18,64,128]{2,1,0:T(8,128)(2,1)S(1)}, bf16[18,64,128]{2,1,0:T(8,128)(2,1)S(1)}) custom-call(s32[4,128]{1,0:T(4,128)S(1)} %pad_add_fusion.req, bf16[8,64,1024]{2,1,0:T(8,128)(2,1)} %v0.1), custom_call_target="tpu_custom_call" | custom-call | tf_op jit(solution)/shard_map/zeta_home/pallas_call | solution.py:99
  54.3 3.7 %collective-permute-start.5 = (bf16[18,64,128]{2,1,0:T(8,128)(2,1)S(1)}, bf16[18,64,128]{2,1,0:T(8,128)(2,1)S(1)}, u32[]{:S(2)}, u32[]{:S(2)}) collective-permute-start(bf16[18,64,128]{2,1,0:T(8,128)(2,1)S(1)} %get-tuple-element.34), channel_id=1, source_target_pairs={{0,96},{32,0},{64,32},{96,64},{1,97},{33,1},{65,33},{97,65},{2,98}... | collective-permute-start | bytes 884744 | tf_op jit(solution)/shard_map/ppermute | solution.py:542
  58.0 1.5 collective-permute-start.9
  59.6 2.6 %collective-permute-start.7 = (bf16[2,64,1024]{2,1,0:T(8,128)(2,1)S(1)}, bf16[2,64,1024]{2,1,0:T(8,128)(2,1)S(1)}, u32[]{:S(2)}, u32[]{:S(2)}) collective-permute-start(bf16[2,64,1024]{2,1,0:T(8,128)(2,1)S(1)} %slice.16), channel_id=1, source_target_pairs={{0,32},{32,64},{64,96},{96,0},{1,33},{33,65},{65,97},{97,1},{2,34}... | collective-permute-start | bytes 786440 | tf_op jit(solution)/shard_map/ppermute | solution.py:542
  62.2 6.6 %collective-permute-done.5.z1 = bf16[18,64,128]{2,1,0:T(8,128)(2,1)S(1)} collective-permute-done((bf16[18,64,128]{2,1,0:T(8,128)(2,1)S(1)}, bf16[18,64,128]{2,1,0:T(8,128)(2,1)S(1)}, u32[]{:S(2)}, u32[]{:S(2)}) %collective-permute-start.5) | collective-permute-done | bytes 294944 | tf_op jit(solution)/shard_map/ppermute | solution.py:542
  68.8 6.0 %collective-permute-done.6.z3 = bf16[18,64,128]{2,1,0:T(8,128)(2,1)S(1)} collective-permute-done((bf16[18,64,128]{2,1,0:T(8,128)(2,1)S(1)}, bf16[18,64,128]{2,1,0:T(8,128)(2,1)S(1)}, u32[]{:S(2)}, u32[]{:S(2)}) %collective-permute-start.6) | collective-permute-done | bytes 294944 | tf_op jit(solution)/shard_map/ppermute | solution.py:542
  74.8 16.6 %pairs_a.1 = (f32[8,64,1024]{2,1,0:T(8,128)S(1)}, bf16[32,64,64]{2,1,0:T(8,128)(2,1)S(1)}, bf16[4,64,1024]{2,1,0:T(8,128)(2,1)S(1)}, s32[128]{0:T(128)S(1)}) custom-call(s32[128]{0:T(128)S(1)} %concatenate.16.meta, bf16[8,64,1024]{2,1,0:T(8,128)(2,1)} %u0.1, bf16[8,64,1024]{2,1,0:T(8,128)(2,1)} %copy-done, bf16[8,64,1024]{2,1,0:T(8,128)(2,1)} %copy-done.3, ...), custom_call_target="tpu_custom_call" | custom-call | tf_op jit(solution)/shard_map/pairs_a/pallas_call | solution.py:273
  92.5 9.9 %pairs_b.1 = (f32[4,64,1024]{2,1,0:T(8,128)S(1)}, f32[4,64,1024]{2,1,0:T(8,128)S(1)}, bf16[32,64,64]{2,1,0:T(8,128)(2,1)S(1)}, bf16[4,64,1024]{2,1,0:T(8,128)(2,1)S(1)}) custom-call(s32[128]{0:T(128)S(1)} %concatenate.16.meta, bf16[2,64,1024]{2,1,0:T(8,128)(2,1)} %copy-done.7, bf16[6,64,1024]{2,1,0:T(8,128)(2,1)} %copy-done.4, ...), custom_call_target="tpu_custom_call" | custom-call | tf_op jit(solution)/shard_map/pairs_b/pallas_call | solution.py:285
  102.7 2.1 %collective-permute-start.26 = (bf16[4,64,1024]{2,1,0:T(8,128)(2,1)S(1)}, bf16[4,64,1024]{2,1,0:T(8,128)(2,1)S(1)}, u32[]{:S(2)}, u32[]{:S(2)}) collective-permute-start(bf16[4,64,1024]{2,1,0:T(8,128)(2,1)S(1)} %slice.18), channel_id=1, source_target_pairs={{0,32},{32,64},{64,96},{96,0},{1,33},{33,65},{65,97},{97,1},{2,34}... | collective-permute-start | bytes 1572872 | tf_op jit(solution)/shard_map/ppermute | solution.py:542
  105.9 5.7 %collective-permute-start.12 = (bf16[64,1024]{1,0:T(8,128)(2,1)S(1)}, bf16[64,1024]{1,0:T(8,128)(2,1)S(1)}, u32[]{:S(2)}, u32[]{:S(2)}) collective-permute-start(bf16[64,1024]{1,0:T(8,128)(2,1)S(1)} %bitcast.13), channel_id=1, source_target_pairs={{0,16},{1,17},{2,18},{3,19},{4,20},{5,21},{6,22},{7,23},{8,24},{9,... | collective-permute-start | bytes 393224 | tf_op jit(solution)/shard_map/ppermute | solution.py:552
  111.8 16.5 %collective-permute-done.24.v1 = bf16[8,64,1024]{2,1,0:T(8,128)(2,1)S(1)} collective-permute-done((bf16[8,64,1024]{2,1,0:T(8,128)(2,1)}, bf16[8,64,1024]{2,1,0:T(8,128)(2,1)S(1)}, u32[]{:S(2)}, u32[]{:S(2)}) %collective-permute-start.24) | collective-permute-done | bytes 1048608 | tf_op jit(solution)/shard_map/ppermute | solution.py:542
  128.3 1.6 collective-permute-start.27
  130.0 1.6 collective-permute-start.14
  131.6 2.1 %collective-permute-start.15 = (bf16[64,1024]{1,0:T(8,128)(2,1)S(1)}, bf16[64,1024]{1,0:T(8,128)(2,1)S(1)}, u32[]{:S(2)}, u32[]{:S(2)}) collective-permute-start(bf16[64,1024]{1,0:T(8,128)(2,1)S(1)} %add4.2.a), channel_id=1, source_target_pairs={{0,4},{1,5},{2,6},{3,7},{4,0},{5,1},{6,2},{7,3},{8,12},{9,13},{10,... | collective-permute-start | bytes 393224 | tf_op jit(solution)/shard_map/ppermute | solution.py:552
  135.0 2.1 %collective-permute-done.14.b = bf16[64,1024]{1,0:T(8,128)(2,1)S(1)} collective-permute-done((bf16[64,1024]{1,0:T(8,128)(2,1)S(1)}, bf16[64,1024]{1,0:T(8,128)(2,1)S(1)}, u32[]{:S(2)}, u32[]{:S(2)}) %collective-permute-start.14) | collective-permute-done | bytes 131104 | tf_op jit(solution)/shard_map/ppermute | solution.py:552
  137.2 2.3 %collective-permute-done.15.c = bf16[64,1024]{1,0:T(8,128)(2,1)S(1)} collective-permute-done((bf16[64,1024]{1,0:T(8,128)(2,1)S(1)}, bf16[64,1024]{1,0:T(8,128)(2,1)S(1)}, u32[]{:S(2)}, u32[]{:S(2)}) %collective-permute-start.15) | collective-permute-done | bytes 131104 | tf_op jit(solution)/shard_map/ppermute | solution.py:552
  139.7 4.9 %collective-permute-start.17 = (bf16[64,1024]{1,0:T(8,128)(2,1)S(1)}, bf16[64,1024]{1,0:T(8,128)(2,1)S(1)}, u32[]{:S(2)}, u32[]{:S(2)}) collective-permute-start(bf16[64,1024]{1,0:T(8,128)(2,1)S(1)} %add4.3.s0), channel_id=1, source_target_pairs={{0,24},{1,25},{2,26},{3,27},{4,28},{5,29},{6,30},{7,31},{8,0},{9,1... | collective-permute-start | bytes 393224 | tf_op jit(solution)/shard_map/ppermute | solution.py:552
  146.6 2.5 %collective-permute-done.17.s1 = bf16[64,1024]{1,0:T(8,128)(2,1)S(1)} collective-permute-done((bf16[64,1024]{1,0:T(8,128)(2,1)S(1)}, bf16[64,1024]{1,0:T(8,128)(2,1)S(1)}, u32[]{:S(2)}, u32[]{:S(2)}) %collective-permute-start.17) | collective-permute-done | bytes 131104 | tf_op jit(solution)/shard_map/ppermute | solution.py:552
  149.2 2.3 %collective-permute-done.18.s2 = bf16[64,1024]{1,0:T(8,128)(2,1)S(1)} collective-permute-done((bf16[64,1024]{1,0:T(8,128)(2,1)S(1)}, bf16[64,1024]{1,0:T(8,128)(2,1)S(1)}, u32[]{:S(2)}, u32[]{:S(2)}) %collective-permute-start.18) | collective-permute-done | bytes 131104 | tf_op jit(solution)/shard_map/ppermute | solution.py:552
  154.2 12.8 %image_part.1 = (f32[16,32,512]{2,1,0:T(8,128)S(1)}, f32[16,32,512]{2,1,0:T(8,128)S(1)}, bf16[8,64,1024]{2,1,0:T(8,128)(2,1)S(1)}) custom-call(s32[128]{0:T(128)S(1)} %concatenate.16.meta, s32[128]{0:T(128)S(1)} %get-tuple-element.36.plan, bf16[64,1024]{1,0:T(8,128)(2,1)S(1)} %add4.3.s0, bf16[64,1024]{1,0:T(8,128)(2,1)S(1)} %collective-permute-done.17.s1, ...), custom_call_target="tpu_custom_call" | custom-call | tf_op jit(solution)/shard_map/image_part/pallas_call | solution.py:380
  167.7 2.3 %collective-permute-done.28.b = f32[16,32,512]{2,1,0:T(8,128)S(1)} collective-permute-done((f32[16,32,512]{2,1,0:T(8,128)S(1)}, f32[16,32,512]{2,1,0:T(8,128)S(1)}, u32[]{:S(2)}, u32[]{:S(2)}) %collective-permute-start.28) | collective-permute-done | bytes 1048608 | tf_op jit(solution)/shard_map/ppermute | solution.py:552
  170.8 1.8 collective-permute-start.30
  172.6 1.7 collective-permute-start.31
  174.2 6.3 %collective-permute-done.29.b = bf16[4,32,512]{2,1,0:T(8,128)(2,1)S(1)} collective-permute-done((bf16[4,32,512]{2,1,0:T(8,128)(2,1)S(1)}, bf16[4,32,512]{2,1,0:T(8,128)(2,1)S(1)}, u32[]{:S(2)}, u32[]{:S(2)}) %collective-permute-start.29) | collective-permute-done | bytes 131104 | tf_op jit(solution)/shard_map/ppermute | solution.py:552
  182.2 2.9 %collective-permute-start.33 = (f32[32,512]{1,0:T(8,128)S(1)}, f32[32,512]{1,0:T(8,128)S(1)}, u32[]{:S(2)}, u32[]{:S(2)}) collective-permute-start(f32[32,512]{1,0:T(8,128)S(1)} %get-tuple-element.60), channel_id=1, source_target_pairs={{0,4},{1,5},{2,6},{3,7},{4,0},{5,1},{6,2},{7,3},{8,12},{9,13},{10,... | collective-permute-start | bytes 196616 | tf_op jit(solution)/shard_map/ppermute | solution.py:552
  185.1 2.2 %collective-permute-start.34 = (f32[32,512]{1,0:T(8,128)S(1)}, f32[32,512]{1,0:T(8,128)S(1)}, u32[]{:S(2)}, u32[]{:S(2)}) collective-permute-start(f32[32,512]{1,0:T(8,128)S(1)} %get-tuple-element.61), channel_id=1, source_target_pairs={{0,6},{1,7},{2,0},{3,1},{4,2},{5,3},{6,4},{7,5},{8,14},{9,15},{10,... | collective-permute-start | bytes 196616 | tf_op jit(solution)/shard_map/ppermute | solution.py:552
  188.3 3.5 %factor_1.1.m_in = f32[8,64,128]{2,1,0:T(8,128)S(1)} custom-call(f32[8,64,128]{2,1,0:T(8,128)S(1)} %factor_0.1.m_in), custom_call_target="tpu_custom_call" | custom-call | tf_op jit(solution)/shard_map/factor_1/pallas_call | solution.py:457
  191.9 6.2 %factor_2.1 = (f32[8,32,64]{2,1,0:T(8,128)}, f32[8,64,64]{2,1,0:T(8,128)S(1)}) custom-call(s32[128]{0:T(128)S(1)} %concatenate.16.meta, bf16[8,64,1024]{2,1,0:T(8,128)(2,1)S(1)} %get-tuple-element.49.s_ref, f32[8,64,128]{2,1,0:T(8,128)S(1)} %factor_1.1.m_in), custom_call_target="tpu_custom_call" | custom-call | tf_op jit(solution)/shard_map/factor_2/pallas_call | solution.py:460
  (77 shorter events, 19.8 us)
Async XLA Ops:
  0.6 25.7 %collective-permute-start = (bf16[8,64,1024]{2,1,0:T(8,128)(2,1)}, bf16[8,64,1024]{2,1,0:T(8,128)(2,1)S(1)}, u32[]{:S(2)}, u32[]{:S(2)}) collective-permute-start(bf16[8,64,1024]{2,1,0:T(8,128)(2,1)} %u0.1), channel_id=1, source_target_pairs={{0,96},{32,0},{64,32},{96,64},{1,97},{33,1},{65,33},{97,65},{2,98}... | collective-permute-start | bytes 3145736 | tf_op jit(solution)/shard_map/ppermute | solution.py:542
  3.6 56.0 %collective-permute-start.1 = (bf16[8,64,1024]{2,1,0:T(8,128)(2,1)}, bf16[8,64,1024]{2,1,0:T(8,128)(2,1)S(1)}, u32[]{:S(2)}, u32[]{:S(2)}) collective-permute-start(bf16[8,64,1024]{2,1,0:T(8,128)(2,1)} %u0.1), channel_id=1, source_target_pairs={{0,32},{32,64},{64,96},{96,0},{1,33},{33,65},{65,97},{97,1},{2,34}... | collective-permute-start | bytes 3145736 | tf_op jit(solution)/shard_map/ppermute | solution.py:542
  27.3 64.2 %collective-permute-start.8 = (bf16[6,64,1024]{2,1,0:T(8,128)(2,1)}, bf16[6,64,1024]{2,1,0:T(8,128)(2,1)S(1)}, u32[]{:S(2)}, u32[]{:S(2)}) collective-permute-start(bf16[6,64,1024]{2,1,0:T(8,128)(2,1)} %slice.17), channel_id=1, source_target_pairs={{0,96},{32,0},{64,32},{96,64},{1,97},{33,1},{65,33},{97,65},{2,98}... | collective-permute-start | bytes 2359304 | tf_op jit(solution)/shard_map/ppermute | solution.py:542
  31.7 15.5 %collective-permute-start.2 = (s32[1,128]{1,0:T(1,128)S(1)}, s32[1,128]{1,0:T(1,128)S(1)}, u32[]{:S(2)}, u32[]{:S(2)}) collective-permute-start(s32[1,128]{1,0:T(1,128)S(1)} %bitcast.16), channel_id=1, source_target_pairs={{0,96},{32,0},{64,32},{96,64},{1,97},{33,1},{65,33},{97,65},{2,98}... | collective-permute-start | bytes 1544 | tf_op jit(solution)/shard_map/ppermute | solution.py:542
  31.7 15.5 %collective-permute-start.3 = (s32[1,128]{1,0:T(1,128)S(1)}, s32[1,128]{1,0:T(1,128)S(1)}, u32[]{:S(2)}, u32[]{:S(2)}) collective-permute-start(s32[1,128]{1,0:T(1,128)S(1)} %bitcast.17), channel_id=1, source_target_pairs={{0,64},{32,96},{64,0},{96,32},{1,65},{33,97},{65,1},{97,33},{2,66}... | collective-permute-start | bytes 1544 | tf_op jit(solution)/shard_map/ppermute | solution.py:542
  32.2 15.0 %collective-permute-start.4 = (s32[1,128]{1,0:T(1,128)S(1)}, s32[1,128]{1,0:T(1,128)S(1)}, u32[]{:S(2)}, u32[]{:S(2)}) collective-permute-start(s32[1,128]{1,0:T(1,128)S(1)} %bitcast.18), channel_id=1, source_target_pairs={{0,32},{32,64},{64,96},{96,0},{1,33},{33,65},{65,97},{97,1},{2,34}... | collective-permute-start | bytes 1544 | tf_op jit(solution)/shard_map/ppermute | solution.py:542
  54.3 14.5 %collective-permute-start.5 = (bf16[18,64,128]{2,1,0:T(8,128)(2,1)S(1)}, bf16[18,64,128]{2,1,0:T(8,128)(2,1)S(1)}, u32[]{:S(2)}, u32[]{:S(2)}) collective-permute-start(bf16[18,64,128]{2,1,0:T(8,128)(2,1)S(1)} %get-tuple-element.34), channel_id=1, source_target_pairs={{0,96},{32,0},{64,32},{96,64},{1,97},{33,1},{65,33},{97,65},{2,98}... | collective-permute-start | bytes 884744 | tf_op jit(solution)/shard_map/ppermute | solution.py:542
  58.0 16.8 %collective-permute-start.6 = (bf16[18,64,128]{2,1,0:T(8,128)(2,1)S(1)}, bf16[18,64,128]{2,1,0:T(8,128)(2,1)S(1)}, u32[]{:S(2)}, u32[]{:S(2)}) collective-permute-start(bf16[18,64,128]{2,1,0:T(8,128)(2,1)S(1)} %get-tuple-element.35), channel_id=1, source_target_pairs={{0,32},{32,64},{64,96},{96,0},{1,33},{33,65},{65,97},{97,1},{2,34}... | collective-permute-start | bytes 884744 | tf_op jit(solution)/shard_map/ppermute | solution.py:542
  58.0 33.4 %collective-permute-start.9 = (bf16[18,64,128]{2,1,0:T(8,128)(2,1)S(1)}, bf16[18,64,128]{2,1,0:T(8,128)(2,1)S(1)}, u32[]{:S(2)}, u32[]{:S(2)}) collective-permute-start(bf16[18,64,128]{2,1,0:T(8,128)(2,1)S(1)} %get-tuple-element.37), channel_id=1, source_target_pairs={{0,64},{32,96},{64,0},{96,32},{1,65},{33,97},{65,1},{97,33},{2,66}... | collective-permute-start | bytes 884744 | tf_op jit(solution)/shard_map/ppermute | solution.py:542
  59.6 31.9 %collective-permute-start.7 = (bf16[2,64,1024]{2,1,0:T(8,128)(2,1)S(1)}, bf16[2,64,1024]{2,1,0:T(8,128)(2,1)S(1)}, u32[]{:S(2)}, u32[]{:S(2)}) collective-permute-start(bf16[2,64,1024]{2,1,0:T(8,128)(2,1)S(1)} %slice.16), channel_id=1, source_target_pairs={{0,32},{32,64},{64,96},{96,0},{1,33},{33,65},{65,97},{97,1},{2,34}... | collective-permute-start | bytes 786440 | tf_op jit(solution)/shard_map/ppermute | solution.py:542
  68.8 33.8 %collective-permute-start.25 = (bf16[8,64,1024]{2,1,0:T(8,128)(2,1)}, bf16[8,64,1024]{2,1,0:T(8,128)(2,1)S(1)}, u32[]{:S(2)}, u32[]{:S(2)}) collective-permute-start(bf16[8,64,1024]{2,1,0:T(8,128)(2,1)} %v0.1), channel_id=1, source_target_pairs={{0,32},{32,64},{64,96},{96,0},{1,33},{33,65},{65,97},{97,1},{2,34}... | collective-permute-start | bytes 3145736 | tf_op jit(solution)/shard_map/ppermute | solution.py:542
  102.5 25.8 %collective-permute-start.24 = (bf16[8,64,1024]{2,1,0:T(8,128)(2,1)}, bf16[8,64,1024]{2,1,0:T(8,128)(2,1)S(1)}, u32[]{:S(2)}, u32[]{:S(2)}) collective-permute-start(bf16[8,64,1024]{2,1,0:T(8,128)(2,1)} %v0.1), channel_id=1, source_target_pairs={{0,96},{32,0},{64,32},{96,64},{1,97},{33,1},{65,33},{97,65},{2,98}... | collective-permute-start | bytes 3145736 | tf_op jit(solution)/shard_map/ppermute | solution.py:542
  102.7 44.0 %collective-permute-start.26 = (bf16[4,64,1024]{2,1,0:T(8,128)(2,1)S(1)}, bf16[4,64,1024]{2,1,0:T(8,128)(2,1)S(1)}, u32[]{:S(2)}, u32[]{:S(2)}) collective-permute-start(bf16[4,64,1024]{2,1,0:T(8,128)(2,1)S(1)} %slice.18), channel_id=1, source_target_pairs={{0,32},{32,64},{64,96},{96,0},{1,33},{33,65},{65,97},{97,1},{2,34}... | collective-permute-start | bytes 1572872 | tf_op jit(solution)/shard_map/ppermute | solution.py:542
  105.8 24.1 %collective-permute-start.11 = (bf16[64,1024]{1,0:T(8,128)(2,1)S(1)}, bf16[64,1024]{1,0:T(8,128)(2,1)S(1)}, u32[]{:S(2)}, u32[]{:S(2)}) collective-permute-start(bf16[64,1024]{1,0:T(8,128)(2,1)S(1)} %bitcast.14), channel_id=1, source_target_pairs={{0,8},{1,9},{2,10},{3,11},{4,12},{5,13},{6,14},{7,15},{8,16},{9,17... | collective-permute-start | bytes 393224 | tf_op jit(solution)/shard_map/ppermute | solution.py:552
  105.9 24.0 %collective-permute-start.12 = (bf16[64,1024]{1,0:T(8,128)(2,1)S(1)}, bf16[64,1024]{1,0:T(8,128)(2,1)S(1)}, u32[]{:S(2)}, u32[]{:S(2)}) collective-permute-start(bf16[64,1024]{1,0:T(8,128)(2,1)S(1)} %bitcast.13), channel_id=1, source_target_pairs={{0,16},{1,17},{2,18},{3,19},{4,20},{5,21},{6,22},{7,23},{8,24},{9,... | collective-permute-start | bytes 393224 | tf_op jit(solution)/shard_map/ppermute | solution.py:552
  111.6 18.3 %collective-permute-start.13 = (bf16[64,1024]{1,0:T(8,128)(2,1)S(1)}, bf16[64,1024]{1,0:T(8,128)(2,1)S(1)}, u32[]{:S(2)}, u32[]{:S(2)}) collective-permute-start(bf16[64,1024]{1,0:T(8,128)(2,1)S(1)} %bitcast.12), channel_id=1, source_target_pairs={{0,24},{1,25},{2,26},{3,27},{4,28},{5,29},{6,30},{7,31},{8,0},{9,1... | collective-permute-start | bytes 393224 | tf_op jit(solution)/shard_map/ppermute | solution.py:552
  128.3 24.6 %collective-permute-start.27 = (bf16[4,64,1024]{2,1,0:T(8,128)(2,1)S(1)}, bf16[4,64,1024]{2,1,0:T(8,128)(2,1)S(1)}, u32[]{:S(2)}, u32[]{:S(2)}) collective-permute-start(bf16[4,64,1024]{2,1,0:T(8,128)(2,1)S(1)} %slice.19), channel_id=1, source_target_pairs={{0,96},{32,0},{64,32},{96,64},{1,97},{33,1},{65,33},{97,65},{2,98}... | collective-permute-start | bytes 1572872 | tf_op jit(solution)/shard_map/ppermute | solution.py:542
  130.0 7.2 %collective-permute-start.14 = (bf16[64,1024]{1,0:T(8,128)(2,1)S(1)}, bf16[64,1024]{1,0:T(8,128)(2,1)S(1)}, u32[]{:S(2)}, u32[]{:S(2)}) collective-permute-start(bf16[64,1024]{1,0:T(8,128)(2,1)S(1)} %add4.2.a), channel_id=1, source_target_pairs={{0,2},{1,3},{2,4},{3,5},{4,6},{5,7},{6,0},{7,1},{8,10},{9,11},{10,... | collective-permute-start | bytes 393224 | tf_op jit(solution)/shard_map/ppermute | solution.py:552
  131.6 7.8 %collective-permute-start.15 = (bf16[64,1024]{1,0:T(8,128)(2,1)S(1)}, bf16[64,1024]{1,0:T(8,128)(2,1)S(1)}, u32[]{:S(2)}, u32[]{:S(2)}) collective-permute-start(bf16[64,1024]{1,0:T(8,128)(2,1)S(1)} %add4.2.a), channel_id=1, source_target_pairs={{0,4},{1,5},{2,6},{3,7},{4,0},{5,1},{6,2},{7,3},{8,12},{9,13},{10,... | collective-permute-start | bytes 393224 | tf_op jit(solution)/shard_map/ppermute | solution.py:552
  133.7 5.9 %collective-permute-start.16 = (bf16[64,1024]{1,0:T(8,128)(2,1)S(1)}, bf16[64,1024]{1,0:T(8,128)(2,1)S(1)}, u32[]{:S(2)}, u32[]{:S(2)}) collective-permute-start(bf16[64,1024]{1,0:T(8,128)(2,1)S(1)} %add4.2.a), channel_id=1, source_target_pairs={{0,6},{1,7},{2,0},{3,1},{4,2},{5,3},{6,4},{7,5},{8,14},{9,15},{10,... | collective-permute-start | bytes 393224 | tf_op jit(solution)/shard_map/ppermute | solution.py:552
  139.7 9.5 %collective-permute-start.17 = (bf16[64,1024]{1,0:T(8,128)(2,1)S(1)}, bf16[64,1024]{1,0:T(8,128)(2,1)S(1)}, u32[]{:S(2)}, u32[]{:S(2)}) collective-permute-start(bf16[64,1024]{1,0:T(8,128)(2,1)S(1)} %add4.3.s0), channel_id=1, source_target_pairs={{0,24},{1,25},{2,26},{3,27},{4,28},{5,29},{6,30},{7,31},{8,0},{9,1... | collective-permute-start | bytes 393224 | tf_op jit(solution)/shard_map/ppermute | solution.py:552
  144.6 6.9 %collective-permute-start.18 = (bf16[64,1024]{1,0:T(8,128)(2,1)S(1)}, bf16[64,1024]{1,0:T(8,128)(2,1)S(1)}, u32[]{:S(2)}, u32[]{:S(2)}) collective-permute-start(bf16[64,1024]{1,0:T(8,128)(2,1)S(1)} %add4.3.s0), channel_id=1, source_target_pairs={{0,16},{1,17},{2,18},{3,19},{4,20},{5,21},{6,22},{7,23},{8,24},{9,... | collective-permute-start | bytes 393224 | tf_op jit(solution)/shard_map/ppermute | solution.py:552
  145.3 7.6 %collective-permute-start.19 = (bf16[64,1024]{1,0:T(8,128)(2,1)S(1)}, bf16[64,1024]{1,0:T(8,128)(2,1)S(1)}, u32[]{:S(2)}, u32[]{:S(2)}) collective-permute-start(bf16[64,1024]{1,0:T(8,128)(2,1)S(1)} %add4.3.s0), channel_id=1, source_target_pairs={{0,8},{1,9},{2,10},{3,11},{4,12},{5,13},{6,14},{7,15},{8,16},{9,17... | collective-permute-start | bytes 393224 | tf_op jit(solution)/shard_map/ppermute | solution.py:552
  146.6 6.2 %collective-permute-start.20 = (bf16[64,1024]{1,0:T(8,128)(2,1)S(1)}, bf16[64,1024]{1,0:T(8,128)(2,1)S(1)}, u32[]{:S(2)}, u32[]{:S(2)}) collective-permute-start(bf16[64,1024]{1,0:T(8,128)(2,1)S(1)} %add4.3.s0), channel_id=1, source_target_pairs={{0,1},{1,0},{2,3},{3,2},{4,5},{5,4},{6,7},{7,6},{8,9},{9,8},{10,11... | collective-permute-start | bytes 393224 | tf_op jit(solution)/shard_map/ppermute | solution.py:552
  149.2 3.7 %collective-permute-start.21 = (bf16[64,1024]{1,0:T(8,128)(2,1)S(1)}, bf16[64,1024]{1,0:T(8,128)(2,1)S(1)}, u32[]{:S(2)}, u32[]{:S(2)}) collective-permute-start(bf16[64,1024]{1,0:T(8,128)(2,1)S(1)} %collective-permute-done.17.s1), channel_id=1, source_target_pairs={{0,1},{1,0},{2,3},{3,2},{4,5},{5,4},{6,7},{7,6},{8,9},{9,8},{10,11... | collective-permute-start | bytes 393224 | tf_op jit(solution)/shard_map/ppermute | solution.py:552
  167.1 3.0 %collective-permute-start.28 = (f32[16,32,512]{2,1,0:T(8,128)S(1)}, f32[16,32,512]{2,1,0:T(8,128)S(1)}, u32[]{:S(2)}, u32[]{:S(2)}) collective-permute-start(f32[16,32,512]{2,1,0:T(8,128)S(1)} %get-tuple-element.53), channel_id=1, source_target_pairs={{0,1},{1,0},{2,3},{3,2},{4,5},{5,4},{6,7},{7,6},{8,9},{9,8},{10,11... | collective-permute-start | bytes 3145736 | tf_op jit(solution)/shard_map/ppermute | solution.py:552
  170.7 9.9 %collective-permute-start.29 = (bf16[4,32,512]{2,1,0:T(8,128)(2,1)S(1)}, bf16[4,32,512]{2,1,0:T(8,128)(2,1)S(1)}, u32[]{:S(2)}, u32[]{:S(2)}) collective-permute-start(bf16[4,32,512]{2,1,0:T(8,128)(2,1)S(1)} %get-tuple-element.55), channel_id=1, source_target_pairs={{0,8},{1,9},{2,10},{3,11},{4,12},{5,13},{6,14},{7,15},{8,16},{9,17... | collective-permute-start | bytes 393224 | tf_op jit(solution)/shard_map/ppermute | solution.py:552
  170.8 9.8 %collective-permute-start.30 = (bf16[4,32,512]{2,1,0:T(8,128)(2,1)S(1)}, bf16[4,32,512]{2,1,0:T(8,128)(2,1)S(1)}, u32[]{:S(2)}, u32[]{:S(2)}) collective-permute-start(bf16[4,32,512]{2,1,0:T(8,128)(2,1)S(1)} %get-tuple-element.56), channel_id=1, source_target_pairs={{0,16},{1,17},{2,18},{3,19},{4,20},{5,21},{6,22},{7,23},{8,24},{9,... | collective-permute-start | bytes 393224 | tf_op jit(solution)/shard_map/ppermute | solution.py:552
  172.6 8.6 %collective-permute-start.31 = (bf16[4,32,512]{2,1,0:T(8,128)(2,1)S(1)}, bf16[4,32,512]{2,1,0:T(8,128)(2,1)S(1)}, u32[]{:S(2)}, u32[]{:S(2)}) collective-permute-start(bf16[4,32,512]{2,1,0:T(8,128)(2,1)S(1)} %get-tuple-element.57), channel_id=1, source_target_pairs={{0,24},{1,25},{2,26},{3,27},{4,28},{5,29},{6,30},{7,31},{8,0},{9,1... | collective-permute-start | bytes 393224 | tf_op jit(solution)/shard_map/ppermute | solution.py:552
  181.8 16.4 %collective-permute-start.32 = (f32[32,512]{1,0:T(8,128)S(1)}, f32[32,512]{1,0:T(8,128)S(1)}, u32[]{:S(2)}, u32[]{:S(2)}) collective-permute-start(f32[32,512]{1,0:T(8,128)S(1)} %get-tuple-element.59), channel_id=1, source_target_pairs={{0,2},{1,3},{2,4},{3,5},{4,6},{5,7},{6,0},{7,1},{8,10},{9,11},{10,... | collective-permute-start | bytes 196616 | tf_op jit(solution)/shard_map/ppermute | solution.py:552
  182.2 15.9 %collective-permute-start.33 = (f32[32,512]{1,0:T(8,128)S(1)}, f32[32,512]{1,0:T(8,128)S(1)}, u32[]{:S(2)}, u32[]{:S(2)}) collective-permute-start(f32[32,512]{1,0:T(8,128)S(1)} %get-tuple-element.60), channel_id=1, source_target_pairs={{0,4},{1,5},{2,6},{3,7},{4,0},{5,1},{6,2},{7,3},{8,12},{9,13},{10,... | collective-permute-start | bytes 196616 | tf_op jit(solution)/shard_map/ppermute | solution.py:552
  185.1 13.0 %collective-permute-start.34 = (f32[32,512]{1,0:T(8,128)S(1)}, f32[32,512]{1,0:T(8,128)S(1)}, u32[]{:S(2)}, u32[]{:S(2)}) collective-permute-start(f32[32,512]{1,0:T(8,128)S(1)} %get-tuple-element.61), channel_id=1, source_target_pairs={{0,6},{1,7},{2,0},{3,1},{4,2},{5,3},{6,4},{7,5},{8,14},{9,15},{10,... | collective-permute-start | bytes 196616 | tf_op jit(solution)/shard_map/ppermute | solution.py:552
  (11 other events, 157.5 us)
where the time goes:
time: 200 us; the launch traced here: 199 us
  waiting for transfers between devices  84.9 us (42%)
  Pallas kernels  60.5 us (30%)
  starting transfers between devices  48 us (24%)
  local copies, waits for them, and re-layouts  3.65 us (2%)
    ppermute x14, waiting for transfers between devices, along_x(): return lax.ppermute(x, 'tgt', [(i, (i + step) % 4) for i in range(4)])  63.1 us
    ppermute x21, starting transfers between devices, along_inner(): return lax.ppermute(x, 'inner', pairs)  27.8 us
    ppermute x21, waiting for transfers between devices, along_inner(): return lax.ppermute(x, 'inner', pairs)  21.8 us
    ppermute x14, starting transfers between devices, along_x(): return lax.ppermute(x, 'tgt', [(i, (i + step) % 4) for i in range(4)])  20.2 us
    pallas_call x1, Pallas kernels, pairs_a(): pl.pallas_call(pairs_a_kernel, out_shape=(ACC, MIX, LEFT, jax.ShapeDtypeS...  16.6 us
    pallas_call x1, Pallas kernels, image_part(): pl.pallas_call(image_kernel, out_shape=(half, half, jax.ShapeDtypeStruct(...  12.8 us
    pallas_call x1, Pallas kernels, pairs_b(): pl.pallas_call(pairs_b_kernel, out_shape=(QUAD, QUAD, MIX, LEFT), in_spec...  9.88 us
    pallas_call x1, Pallas kernels, zeta_home(): pl.pallas_call(zeta_kernel, out_shape=(out,) * 4, in_specs=[SMEM, VM], ou...  7.1 us
  transfers between devices with their start and end apart: 35, of which 16 were waited for; matrix products, arithmetic and copies ran while one was open for 2% of the time, Pallas kernels for 23%

commit v1 on v0

--- a/solution.py
+++ b/solution.py
@@ -111,7 +111,7 @@
     )(req, v_own)
 
 
-PLUS_TILES = 2
+PLUS_TILES = 4
 
 
 def start_tile(r, own, dst, sem):
@@ -122,42 +122,64 @@
             pltpu.make_async_copy(ref.at[(r & 7) - shift], dst, sem).start()
 
 
-def build_plan(meta, plan):
-    def per_target(t, slot):
-        def per_pair(j, at):
-            hit = meta[M_T + j] == t
-
-            @pl.when(hit)
-            def _():
-                plan[at] = j + 256
-
-            return at + hit.astype(jnp.int32)
-
-        end = lax.fori_loop(0, N_LOW, per_pair, slot)
-        full = (end + 3) // 4 * 4
-
-        @pl.when(end > slot)
-        def _():
-            plan[64 + slot // 4] = t
-
-            def more(c, carry):
-                plan[64 + c] = t
-                return carry
-
-            lax.fori_loop(slot // 4, full // 4, more, 0)
-
-            def pad(i, carry):
-                plan[i] = plan[end - 1] & 255
-                return carry
-
-            lax.fori_loop(end, full, pad, 0)
-
-        return full
-
-    plan[127] = lax.fori_loop(0, 8, per_target, 0)
-
-
-def pairs_body(meta, mine, own, zbuf, lv, lu, nt, mix, lt, acc, lst, lvb, lub, ub, nb, unb, sems, nsems):
+def plan_kernel(meta, plan, count, place):
+    for t in range(8):
+        count[t] = 0
+
+    def tally(j, carry):
+        t = meta[M_T + j]
+        count[t] = count[t] + 1
+        return carry
+
+    lax.fori_loop(0, N_LOW, tally, 0)
+
+    def start(t, slot):
+        place[t] = slot
+        full = (count[t] + 3) // 4
+
+        def mark(c, carry):
+            plan[64 + slot // 4 + c] = t
+            return carry
+
+        lax.fori_loop(0, full, mark, 0)
+        return slot + full * 4
+
+    plan[127] = lax.fori_loop(0, 8, start, 0)
+
+    def put(j, carry):
+        t = meta[M_T + j]
+        at = place[t]
+        plan[at] = j + 256
+        place[t] = at + 1
+        return carry
+
+    lax.fori_loop(0, N_LOW, put, 0)
+
+    def pad(t, carry):
+        end = place[t]
+
+        def fill(i, carry):
+            plan[i] = plan[end - 1] & 255
+            return carry
+
+        return lax.fori_loop(end, (end + 3) // 4 * 4, fill, carry)
+
+    lax.fori_loop(0, 8, pad, 0)
+
+
+def make_plan(meta):
+    return pl.pallas_call(
+        plan_kernel,
+        out_shape=jax.ShapeDtypeStruct((128,), jnp.int32),
+        in_specs=[SMEM],
+        out_specs=SMEM,
+        scratch_shapes=[pltpu.SMEM((8,), jnp.int32), pltpu.SMEM((8,), jnp.int32)],
+        compiler_params=SMALL,
+        name="make_plan",
+    )(meta)
+
+
+def left_body(meta, mine, own, lv, nt, mix, lt, lst, lvb, ub, nb, unb, sems, nsems):
     def low(j, n):
         r = meta[j]
         hit = mine(r >> 3)
@@ -167,7 +189,6 @@
             lst[n] = j
             pltpu.make_async_copy(lv.at[j], lvb.at[n], sems.at[0, n]).start()
             start_tile(r, own, ub.at[n], sems.at[1, n])
-            pltpu.make_async_copy(lu.at[j], lub.at[n], sems.at[2, n]).start()
 
         return n + hit.astype(jnp.int32)
 
@@ -187,66 +208,129 @@
 
     nn = lax.fori_loop(0, N_NEAR, near, 0)
 
+    def group(g, carry):
+        for i in range(4):
+            pos = g * 4 + i
+
+            @pl.when(pos < n)
+            def _():
+                pltpu.make_async_copy(lv.at[0], lvb.at[pos], sems.at[0, pos]).wait()
+                pltpu.make_async_copy(lv.at[0], ub.at[pos], sems.at[1, pos]).wait()
+
+        spots = [jnp.minimum(g * 4 + i, n - 1) for i in range(4)]
+        done = [dot_nt(ub[pos], lvb[pos]).astype(BF16) for pos in spots]
+        for pos, mt in zip(spots, done):
+            mix[lst[pos]] = mt
+        return carry
+
+    lax.fori_loop(0, (n + 3) // 4, group, 0)
+
+    def tile(m, carry):
+        pltpu.make_async_copy(nt.at[0], nb.at[m], nsems.at[0, m]).wait()
+        pltpu.make_async_copy(lv.at[0], unb.at[m], nsems.at[1, m]).wait()
+        lt[lst[N_LOW + m]] = dot_nt(unb[m], nb[m]).astype(BF16)
+        return carry
+
+    lax.fori_loop(0, nn, tile, 0)
+
+
+def sum_body(meta, mine, zbuf, lu, mix, lt, acc, lst, lub, sems):
+    def low(j, n):
+        hit = mine(meta[j] >> 3)
+
+        @pl.when(hit)
+        def _():
+            lst[n] = j
+            pltpu.make_async_copy(lu.at[j], lub.at[n], sems.at[n]).start()
+
+        return n + hit.astype(jnp.int32)
+
+    n = lax.fori_loop(0, N_LOW, low, 0)
+
     def zeta(j):
         second = j >= HALF
         blk = zbuf[meta[j] >> 3, jnp.where(second, j - HALF, j)].astype(F32)
         return jnp.where(second, pltpu.roll(blk, R, 1), blk)[:, :R].astype(BF16)
 
+    def tile(s, carry):
+        @pl.when(mine(meta[N_LOW + s] >> 3))
+        def _():
+            acc[meta[M_T + N_LOW + s]] += dot_nn(zeta(N_LOW + s), lt[s])
+
+        return carry
+
+    lax.fori_loop(0, meta[M_COUNT], tile, 0)
+
     def group(g, carry):
+        terms = []
+        for i in range(4):
+            pos = jnp.minimum(g * 4 + i, n - 1)
+            j = lst[pos]
+            hi, lo = split2(dot_nn(zeta(j), mix[j]) * (g * 4 + i < n).astype(F32))
+            terms.append((pos, j, jnp.concatenate([hi, lo], axis=0)))
         for i in range(4):
             pos = g * 4 + i
 
             @pl.when(pos < n)
             def _():
-                pltpu.make_async_copy(lv.at[0], lvb.at[pos], sems.at[0, pos]).wait()
-                pltpu.make_async_copy(lv.at[0], ub.at[pos], sems.at[1, pos]).wait()
-                pltpu.make_async_copy(lu.at[0], lub.at[pos], sems.at[2, pos]).wait()
-
-        for i in range(4):
-            valid = (g * 4 + i < n).astype(F32)
-            pos = jnp.minimum(g * 4 + i, n - 1)
-            j = lst[pos]
-            mt = dot_nt(ub[pos], lvb[pos]).astype(BF16)
-            mix[j] = mt
-            hi, lo = split2(dot_nn(zeta(j), mt) * valid)
-            res = dot_nn(jnp.concatenate([hi, lo], axis=0), lub[pos])
+                pltpu.make_async_copy(lu.at[0], lub.at[pos], sems.at[pos]).wait()
+
+        for pos, j, w in terms:
+            res = dot_nn(w, lub[pos])
             acc[meta[M_T + j]] += res[:R] + res[R:]
         return carry
 
     lax.fori_loop(0, (n + 3) // 4, group, 0)
 
-    def tile(m, carry):
-        s = lst[N_LOW + m]
-        pltpu.make_async_copy(nt.at[0], nb.at[m], nsems.at[0, m]).wait()
-        pltpu.make_async_copy(lv.at[0], unb.at[m], nsems.at[1, m]).wait()
-        left = dot_nt(unb[m], nb[m]).astype(BF16)
-        lt[s] = left
-        acc[meta[M_T + N_LOW + s]] += dot_nn(zeta(N_LOW + s), left)
-        return carry
-
-    lax.fori_loop(0, nn, tile, 0)
-
-
-def pairs_a_kernel(meta, u0, u1, u3, z0, z1, z3, lv, lu, nt, acc, mix, lt, plan, zbuf, *scratch):
-    def own(r):
-        rel = r >> 3
-        return ((rel == 0, u0, 0), (rel == 1, u1, 0), (rel == 3, u3, 0))
-
+
+N_LEFT = 7
+
+
+def pairs_0_kernel(meta, u0, z0, lv, lu, nt, acc, mix, lt, zbuf, *scratch):
     acc[...] = jnp.zeros_like(acc)
-    for n, ref in ((0, z0), (1, z1), (3, z3)):
-        zbuf[n] = ref[...]
-    pairs_body(meta, lambda rel: rel != 2, own, zbuf, lv, lu, nt, mix, lt, acc, *scratch)
-    build_plan(meta, plan)
-
-
-def pairs_b_kernel(meta, u2a, u2b, z2, acc_in, lv, lu, nt, keep, send, mix, lt, zbuf, acc, *scratch):
+    zbuf[0] = z0[...]
+    mine = lambda rel: rel == 0
+    left_body(meta, mine, lambda r: ((r >= 0, u0, 0),), lv, nt, mix, lt, *scratch[:N_LEFT])
+    sum_body(meta, mine, zbuf, lu, mix, lt, acc, *scratch[N_LEFT:])
+
+
+def near_side(rel):
+    return (rel == 1) | (rel == 3)
+
+
+def far_side(rel):
+    return rel == 2
+
+
+def left_a_kernel(meta, u1, u3, mix_in, lt_in, lv, nt, mix, lt, *scratch):
+    mix[...] = mix_in[...]
+    lt[...] = lt_in[...]
+    left_body(
+        meta, near_side, lambda r: ((r < 16, u1, 0), (r >= 16, u3, 0)), lv, nt, mix, lt, *scratch
+    )
+
+
+def left_b_kernel(meta, u2a, u2b, mix_in, lt_in, lv, nt, mix, lt, *scratch):
     def own(r):
         first = (r & 7) < PLUS_TILES
         return ((first, u2a, 0), (jnp.logical_not(first), u2b, PLUS_TILES))
 
+    mix[...] = mix_in[...]
+    lt[...] = lt_in[...]
+    left_body(meta, far_side, own, lv, nt, mix, lt, *scratch)
+
+
+def sum_a_kernel(meta, z1, z3, acc_in, mix, lt, lu, acc, zbuf, *scratch):
+    acc[...] = acc_in[...]
+    zbuf[1] = z1[...]
+    zbuf[3] = z3[...]
+    sum_body(meta, near_side, zbuf, lu, mix, lt, acc, *scratch)
+
+
+def sum_b_kernel(meta, z2, acc_in, mix, lt, lu, keep, send, zbuf, acc, *scratch):
     acc[...] = acc_in[...]
     zbuf[2] = z2[...]
-    pairs_body(meta, lambda rel: rel == 2, own, zbuf, lv, lu, nt, mix, lt, acc, *scratch)
+    sum_body(meta, far_side, zbuf, lu, mix, lt, acc, *scratch)
     core = meta[M_CORE]
     keep[...] = acc[pl.ds(core * 4, 4)]
     send[...] = acc[pl.ds(4 - core * 4, 4)]
@@ -256,50 +340,129 @@
 MIX = jax.ShapeDtypeStruct((N_LOW, R, R), BF16)
 LEFT = jax.ShapeDtypeStruct((N_NEAR, R, B), BF16)
 QUAD = jax.ShapeDtypeStruct((4, R, B), F32)
-PAIR_SCRATCH = [
+LEFT_SCRATCH = [
     pltpu.SMEM((N_PAIR,), jnp.int32),
-    pltpu.VMEM((N_LOW, R, B), BF16),
     pltpu.VMEM((N_LOW, R, B), BF16),
     pltpu.VMEM((N_LOW, R, B), BF16),
     pltpu.VMEM((N_NEAR, B, B), BF16),
     pltpu.VMEM((N_NEAR, R, B), BF16),
-    pltpu.SemaphoreType.DMA((3, N_LOW)),
+    pltpu.SemaphoreType.DMA((2, N_LOW)),
     pltpu.SemaphoreType.DMA((2, N_NEAR)),
 ]
+SUM_SCRATCH = [
+    pltpu.SMEM((N_LOW,), jnp.int32),
+    pltpu.VMEM((N_LOW, R, B), BF16),
+    pltpu.SemaphoreType.DMA((N_LOW,)),
+]
 ZBUF = pltpu.VMEM((4, HALF, R, 128), BF16)
 
 
-def pairs_a(meta, us, zs, low_v, low_u, near):
-    return pl.pallas_call(
-        pairs_a_kernel,
-        out_shape=(ACC, MIX, LEFT, jax.ShapeDtypeStruct((128,), jnp.int32)),
-        in_specs=[SMEM] + [ANY] * 3 + [VM] * 3 + [ANY] * 3,
-        out_specs=(VM, VM, VM, SMEM),
-        scratch_shapes=[ZBUF] + PAIR_SCRATCH,
+def pairs_0(meta, u0, z0, low_v, low_u, near):
+    return pl.pallas_call(
+        pairs_0_kernel,
+        out_shape=(ACC, MIX, LEFT),
+        in_specs=[SMEM, ANY, VM] + [ANY] * 3,
+        out_specs=(VM, VM, VM),
+        scratch_shapes=[ZBUF] + LEFT_SCRATCH + SUM_SCRATCH,
         compiler_params=PARAMS,
-        name="pairs_a",
-    )(meta, *in_hbm(*us), *zs, *in_hbm(low_v, low_u, near))
-
-
-def pairs_b(meta, us, z2, acc, low_v, low_u, near):
-    return pl.pallas_call(
-        pairs_b_kernel,
-        out_shape=(QUAD, QUAD, MIX, LEFT),
-        in_specs=[SMEM] + [ANY] * 2 + [VM, VM] + [ANY] * 3,
-        out_specs=(VM,) * 4,
-        scratch_shapes=[ZBUF, pltpu.VMEM((8, R, B), F32)] + PAIR_SCRATCH,
+        name="pairs_0",
+    )(meta, *in_hbm(u0), z0, *in_hbm(low_v, low_u, near))
+
+
+def left_part(kernel, meta, us, mix, lt, low_v, near):
+    return pl.pallas_call(
+        kernel,
+        out_shape=(MIX, LEFT),
+        in_specs=[SMEM] + [ANY] * 2 + [VM] * 2 + [ANY] * 2,
+        out_specs=(VM, VM),
+        scratch_shapes=LEFT_SCRATCH,
         compiler_params=PARAMS,
-        name="pairs_b",
-    )(meta, *in_hbm(*us), z2, acc, *in_hbm(low_v, low_u, near))
+    )(meta, *in_hbm(*us), mix, lt, *in_hbm(low_v, near))
+
+
+def sum_a(meta, z1, z3, acc, mix, lt, low_u):
+    return pl.pallas_call(
+        sum_a_kernel,
+        out_shape=ACC,
+        in_specs=[SMEM] + [VM] * 5 + [ANY],
+        out_specs=VM,
+        scratch_shapes=[ZBUF] + SUM_SCRATCH,
+        compiler_params=PARAMS,
+        name="sum_a",
+    )(meta, z1, z3, acc, mix, lt, *in_hbm(low_u))
+
+
+def sum_b(meta, z2, acc, mix, lt, low_u):
+    return pl.pallas_call(
+        sum_b_kernel,
+        out_shape=(QUAD, QUAD),
+        in_specs=[SMEM] + [VM] * 4 + [ANY],
+        out_specs=(VM, VM),
+        scratch_shapes=[ZBUF, pltpu.VMEM((8, R, B), F32)] + SUM_SCRATCH,
+        compiler_params=PARAMS,
+        name="sum_b",
+    )(meta, z2, acc, mix, lt, *in_hbm(low_u))
 
 
 SLOTS = 56
 
 
-def image_kernel(
-    meta, plan, s0, s1, s2, s3, r0, r1, r2, r3, v0, v1, v2a, v2b, v3, lu, mixa, mixb, lta, ltb,
-    keep, send, sall, lub, vb, nvb, acc, sems, nsems
+def proj_kernel(
+    meta, plan, s0, s1, s2, s3, r0, r1, r2, r3, lu, mix, lt, p_ref, pn_ref, sall, lub, sems
 ):
+    count = plan[127]
+
+    def load(i, carry):
+        pltpu.make_async_copy(lu.at[plan[i] & 255], lub.at[i], sems.at[i]).start()
+        return carry
+
+    lax.fori_loop(0, count, load, 0)
+    core = meta[M_CORE]
+    z = meta[M_Z]
+    for n, ref in enumerate((s0, s1, s2, s3)):
+        sall[core * 4 + ((z + n) & 3)] = ref[...]
+    for n, ref in enumerate((r0, r1, r2, r3)):
+        sall[(1 - core) * 4 + ((z + n) & 3)] = ref[...]
+
+    for s in range(N_NEAR):
+        hi, lo = split2(dot_nt(sall[meta[M_T + N_LOW + s]], lt[s]))
+        pn_ref[s] = jnp.concatenate([hi, lo], axis=0)
+    n = count // 4
+
+    def ready(m):
+        @pl.when(m < n)
+        def _():
+            for i in range(4):
+                at = m * 4 + i
+                pltpu.make_async_copy(lu.at[0], lub.at[at], sems.at[at]).wait()
+
+    def chunk(m):
+        at = m * 4
+        q = dot_nt(lub[pl.ds(at, 4)].reshape(4 * R, B), sall[plan[64 + m]])
+        parts = []
+        for i in range(4):
+            e = plan[at + i]
+            hi, lo = split2(q[i * R : (i + 1) * R])
+            both = dot_nn(mix[e & 255], jnp.concatenate([hi, lo], axis=1))
+            parts.append((both[:, :R] + both[:, R:]) * (e >> 8).astype(F32))
+        hi, lo = split2(jnp.concatenate(parts, axis=0).T)
+        return jnp.concatenate([hi, lo], axis=0)
+
+    def two(i, carry):
+        m0 = 2 * i
+        m1 = jnp.minimum(m0 + 1, n - 1)
+        ready(m0)
+        ready(m0 + 1)
+        p0 = chunk(m0)
+        p1 = chunk(m1)
+        p_ref[m0] = p0
+        p_ref[m1] = p1
+        return carry
+
+    lax.fori_loop(0, (n + 1) // 2, two, 0)
+
+
+def image_kernel(meta, plan, p_ref, pn_ref, v0, v1, v2a, v2b, v3, keep, send, vb, nvb, acc, sems, nsems):
     def own(r):
         rel = r >> 3
         low = (r & 7) < 4
@@ -314,85 +477,74 @@
     count = plan[127]
 
     def load(i, carry):
-        j = plan[i] & 255
-        pltpu.make_async_copy(lu.at[j], lub.at[i], sems.at[0, i]).start()
-        start_tile(meta[j], own, vb.at[i], sems.at[1, i])
+        start_tile(meta[plan[i] & 255], own, vb.at[i], sems.at[i])
         return carry
 
     lax.fori_loop(0, count, load, 0)
-    live = meta[M_COUNT]
 
     def nload(s, carry):
         start_tile(meta[N_LOW + s], own, nvb.at[s], nsems.at[s])
         return carry
 
-    lax.fori_loop(0, live, nload, 0)
+    lax.fori_loop(0, meta[M_COUNT], nload, 0)
     acc[...] = jnp.zeros_like(acc)
-    core = meta[M_CORE]
-    z = meta[M_Z]
-    for n, ref in enumerate((s0, s1, s2, s3)):
-        sall[core * 4 + ((z + n) & 3)] = ref[...]
-    for n, ref in enumerate((r0, r1, r2, r3)):
-        sall[(1 - core) * 4 + ((z + n) & 3)] = ref[...]
 
     def chunk(m, carry):
         at = m * 4
         for i in range(4):
-            pltpu.make_async_copy(lu.at[0], lub.at[at + i], sems.at[0, at + i]).wait()
-        t = plan[64 + m]
-        q = dot_nt(lub[pl.ds(at, 4)].reshape(4 * R, B), sall[t])
-        parts = []
-        for i in range(4):
-            e = plan[at + i]
-            j = e & 255
-            mt = jnp.where((meta[j] >> 3) == 2, mixb[j], mixa[j])
-            hi, lo = split2(q[i * R : (i + 1) * R])
-            both = dot_nn(mt, jnp.concatenate([hi, lo], axis=1))
-            parts.append((both[:, :R] + both[:, R:]) * (e >> 8).astype(F32))
-        p = jnp.concatenate(parts, axis=0).T
-        hi, lo = split2(p)
-        for i in range(4):
-            pltpu.make_async_copy(lu.at[0], vb.at[at + i], sems.at[1, at + i]).wait()
-        res = dot_nn(jnp.concatenate([hi, lo], axis=0), vb[pl.ds(at, 4)].reshape(4 * R, B))
-        acc[t] += res[:R] + res[R:]
+            pltpu.make_async_copy(v0.at[0], vb.at[at + i], sems.at[at + i]).wait()
+        res = dot_nn(p_ref[m], vb[pl.ds(at, 4)].reshape(4 * R, B))
+        acc[plan[64 + m]] += res[:R] + res[R:]
         return carry
 
     lax.fori_loop(0, count // 4, chunk, 0)
 
     def near(s, carry):
-        t = meta[M_T + N_LOW + s]
-        left = jnp.where((meta[N_LOW + s] >> 3) == 2, ltb[s], lta[s])
-        hi, lo = split2(dot_nt(sall[t], left))
-        pltpu.make_async_copy(lu.at[0], nvb.at[s], nsems.at[s]).wait()
-        res = dot_nn(jnp.concatenate([hi, lo], axis=0), nvb[s])
-        acc[t] += res[:R] + res[R:]
-        return carry
-
-    lax.fori_loop(0, live, near, 0)
+        pltpu.make_async_copy(v0.at[0], nvb.at[s], nsems.at[s]).wait()
+        res = dot_nn(pn_ref[s], nvb[s])
+        acc[meta[M_T + N_LOW + s]] += res[:R] + res[R:]
+        return carry
+
+    lax.fori_loop(0, meta[M_COUNT], near, 0)
     flip = acc[...].reshape(8 * R, B).T.reshape(16, 2, 32, 8 * R)
-    first = core == 0
+    first = meta[M_CORE] == 0
     keep[...] = jnp.where(first, flip[:, 0], flip[:, 1])
     send[...] = jnp.where(first, flip[:, 1], flip[:, 0])
 
 
-def image_part(meta, plan, tiles, vs, low_u, mixes, lefts):
+def proj_part(meta, plan, tiles, low_u, mix, lt):
+    return pl.pallas_call(
+        proj_kernel,
+        out_shape=(
+            jax.ShapeDtypeStruct((SLOTS // 4, 2 * R, 4 * R), BF16),
+            jax.ShapeDtypeStruct((N_NEAR, 2 * R, R), BF16),
+            jax.ShapeDtypeStruct((8, R, B), BF16),
+        ),
+        in_specs=[SMEM, SMEM] + [VM] * 8 + [ANY] + [VM] * 2,
+        out_specs=(VM,) * 3,
+        scratch_shapes=[pltpu.VMEM((SLOTS, R, B), BF16), pltpu.SemaphoreType.DMA((SLOTS,))],
+        compiler_params=PARAMS,
+        name="proj_part",
+    )(meta, plan, *tiles, *in_hbm(low_u), mix, lt)
+
+
+def image_part(meta, plan, p, pn, vs):
     half = jax.ShapeDtypeStruct((16, 32, 8 * R), F32)
     return pl.pallas_call(
         image_kernel,
-        out_shape=(half, half, jax.ShapeDtypeStruct((8, R, B), BF16)),
-        in_specs=[SMEM, SMEM] + [VM] * 8 + [ANY] * 6 + [VM] * 4,
-        out_specs=(VM,) * 3,
+        out_shape=(half, half),
+        in_specs=[SMEM, SMEM, VM, VM] + [ANY] * 5,
+        out_specs=(VM,) * 2,
         scratch_shapes=[
-            pltpu.VMEM((SLOTS, R, B), BF16),
             pltpu.VMEM((SLOTS, R, B), BF16),
             pltpu.VMEM((N_NEAR, R, B), BF16),
             pltpu.VMEM((8, R, B), F32),
-            pltpu.SemaphoreType.DMA((2, SLOTS)),
+            pltpu.SemaphoreType.DMA((SLOTS,)),
             pltpu.SemaphoreType.DMA((N_NEAR,)),
         ],
         compiler_params=PARAMS,
         name="image_part",
-    )(meta, plan, *tiles, *in_hbm(*vs, low_u), *mixes, *lefts)
+    )(meta, plan, p, pn, *in_hbm(*vs))
 
 
 def dot_exact(a, b):
@@ -414,14 +566,17 @@
         m[:, r0:, :] = block - fac * scaled
 
 
-def factor_0_kernel(s_ref, m):
+def factor_0_kernel(meta, s_ref, m, cols):
     lane = lax.broadcasted_iota(jnp.int32, (R, 2 * R), 1)
     row = lax.broadcasted_iota(jnp.int32, (R, 2 * R), 0)
     eye = (lane == row + R).astype(F32)
+    pick_row = lax.broadcasted_iota(jnp.int32, (32, B), 0) + meta[M_S] * 32
+    pick = (lax.broadcasted_iota(jnp.int32, (32, B), 1) == pick_row).astype(BF16)
     for t in range(8):
         s = s_ref[t]
-        g = dot_nt(s, s)
-        m[t] = jnp.where(lane < R, jnp.concatenate([g, g], axis=1), eye)
+        g = dot_nt(jnp.concatenate([s, pick], axis=0), s)
+        m[t] = jnp.where(lane < R, jnp.concatenate([g[:R], g[:R]], axis=1), eye)
+        cols[t] = g[R:]
     eliminate(m, range(CUT0))
 
 
@@ -430,42 +585,46 @@
     eliminate(m, range(CUT0, CUT1))
 
 
-def factor_2_kernel(meta, s_ref, m_in, basis, inv, m):
+def factor_2_kernel(m_in, cols, basis, inv, m):
     m[...] = m_in[...]
     eliminate(m, range(CUT1, R))
     lane = lax.broadcasted_iota(jnp.int32, (R, 2 * R), 1)
     row = lax.broadcasted_iota(jnp.int32, (R, 2 * R), 0)
-    pick_row = lax.broadcasted_iota(jnp.int32, (32, B), 0) + meta[M_S] * 32
-    pick = (lax.broadcasted_iota(jnp.int32, (32, B), 1) == pick_row).astype(BF16)
     for t in range(8):
         a = m[t]
         diag = jnp.sum(jnp.where(lane == row, a, 0.0), axis=1, keepdims=True)
         li = a[:, R:] * lax.rsqrt(diag)
         inv[t] = li
-        basis[t] = 32.0 * dot_exact(dot_nt(pick, s_ref[t]), li)
-
-
-CUT0 = 6
-CUT1 = 36
+        basis[t] = 32.0 * dot_exact(cols[t], li)
+
+
+CUT0 = 8
+CUT1 = 48
 STATE = jax.ShapeDtypeStruct((8, R, 2 * R), F32)
+COLS = jax.ShapeDtypeStruct((8, 32, R), F32)
 
 
 def factor(meta, s):
-    m = pl.pallas_call(
-        factor_0_kernel, out_shape=STATE, in_specs=[VM], out_specs=VM, compiler_params=SMALL, name="factor_0"
-    )(s)
+    m, cols = pl.pallas_call(
+        factor_0_kernel,
+        out_shape=(STATE, COLS),
+        in_specs=[SMEM, VM],
+        out_specs=(VM, VM),
+        compiler_params=SMALL,
+        name="factor_0",
+    )(meta, s)
     m = pl.pallas_call(
         factor_1_kernel, out_shape=STATE, in_specs=[VM], out_specs=VM, compiler_params=SMALL, name="factor_1"
     )(m)
     return pl.pallas_call(
         factor_2_kernel,
-        out_shape=(jax.ShapeDtypeStruct((8, 32, R), F32), jax.ShapeDtypeStruct((8, R, R), F32)),
-        in_specs=[SMEM, VM, VM],
+        out_shape=(COLS, jax.ShapeDtypeStruct((8, R, R), F32)),
+        in_specs=[VM, VM],
         out_specs=(VM, VM),
         scratch_shapes=[pltpu.VMEM((8, R, 2 * R), F32)],
         compiler_params=SMALL,
         name="factor_2",
-    )(meta, s, m)
+    )(m, cols)
 
 
 def first_sum(meta, a, b):
@@ -499,7 +658,6 @@
         in_specs=[VM] * 4,
         out_specs=VM,
         compiler_params=SMALL,
-        name="add4",
     )(a, b, c, d)
 
 
@@ -581,8 +739,13 @@
     v3 = along_x(right_v, 1)
     v1 = along_x(right_v, 3)
 
-    acc, mixa, lta, plan = pairs_a(meta, (right_u, u1, u3), (o0, z1, z3), low_v, low_u, near_tiles)
-    keep, send, mixb, ltb = pairs_b(meta, (u2a, u2b), z2, acc, low_v, low_u, near_tiles)
+    acc, mix, lt = pairs_0(meta, right_u, o0, low_v, low_u, near_tiles)
+    mix, lt = left_part(left_a_kernel, meta, (u1, u3), mix, lt, low_v, near_tiles)
+    acc = sum_a(meta, z1, z3, acc, mix, lt, low_u)
+    mix, lt = left_part(left_b_kernel, meta, (u2a, u2b), mix, lt, low_v, near_tiles)
+    keep, send = sum_b(meta, z2, acc, mix, lt, low_u)
+
+    plan = make_plan(after(meta, keep))
 
     other = along_inner(send, dc=1)
     own, p1, p2, p3 = first_sum(meta, keep, other)
@@ -595,9 +758,8 @@
     mine = (tile, along_inner(tile, dz=3), along_inner(tile, dz=2), along_inner(tile, dz=1))
     theirs = tuple(along_inner(x, dc=1) for x in mine)
 
-    ikeep, isend, sall = image_part(
-        meta, plan, mine + theirs, (right_v, v1, v2a, v2b, v3), low_u, (mixa, mixb), (lta, ltb)
-    )
+    p, pn, sall = proj_part(meta, plan, mine + theirs, low_u, mix, lt)
+    ikeep, isend = image_part(meta, plan, p, pn, (right_v, v1, v2a, v2b, v3))
     basis, inv = factor(meta, sall)
 
     iother = along_inner(isend, dc=1)

time: 200 us -> 174 us (0.87)
  waiting for transfers between devices: 84.9 us -> 54.9 us
  local copies, waits for them, and re-layouts: 3.65 us -> 7.2 us
    ppermute x14, waiting for transfers between devices: 63.1 us -> 34.4 us  [along_x(): return lax.ppermute(x, 'tgt', [(i, (i + step) % 4) for i in range(4)])]
    unnamed x16 -> x20, local copies, waits for them, and re-layouts: 1 us -> 3.78 us
    pallas_call x5 -> x10, Pallas kernels: 46.6 us -> 45.9 us  [the longest x2 10 us: left_part(): pl.pallas_call(kernel, out_shape=(MIX, LEFT), in_specs=[SMEM] + [ANY] * 2...]
  transfers between devices with their start and end apart: 35 -> 35, of which waited for: 16 -> 12; matrix products, arithmetic and copies ran while one was open for 2% -> 2% of each run, Pallas kernels for 23% -> 28%
where the time goes in v1:
time: 174 us
  Pallas kernels  59.9 us (34%)
  waiting for transfers between devices  54.9 us (32%)
  starting transfers between devices  49.2 us (28%)
  local copies, waits for them, and re-layouts  7.2 us (4%)
    ppermute x14, waiting for transfers between devices, along_x(): return lax.ppermute(x, 'tgt', [(i, (i + step) % 4) for i in range(4)])  34.4 us
    ppermute x21, starting transfers between devices, along_inner(): return lax.ppermute(x, 'inner', pairs)  28.5 us
    ppermute x14, starting transfers between devices, along_x(): return lax.ppermute(x, 'tgt', [(i, (i + step) % 4) for i in range(4)])  20.7 us
    ppermute x21, waiting for transfers between devices, along_inner(): return lax.ppermute(x, 'inner', pairs)  20.6 us
    pallas_call x2, Pallas kernels, left_part(): pl.pallas_call(kernel, out_shape=(MIX, LEFT), in_specs=[SMEM] + [ANY] * 2...  10 us
    pallas_call x1, Pallas kernels, proj_part(): pl.pallas_call(proj_kernel, out_shape=(jax.ShapeDtypeStruct((SLOTS // 4,...  7.53 us
    pallas_call x1, Pallas kernels, pairs_0(): pl.pallas_call(pairs_0_kernel, out_shape=(ACC, MIX, LEFT), in_specs=[SMEM...  6.91 us
    pallas_call x1, Pallas kernels, zeta_home(): pl.pallas_call(zeta_kernel, out_shape=(out,) * 4, in_specs=[SMEM, VM], ou...  6.32 us
  transfers between devices with their start and end apart: 35, of which 12 were waited for; matrix products, arithmetic and copies ran while one was open for 2% of the time, Pallas kernels for 28%

profile of v1, /device:TPU:0, one launch (start us, length us, event | category | flops | bytes accessed | tf_op | source)
XLA Modules:
  0.0 173.6 jit_solution(4399460534628926360)
XLA Ops:
  3.9 23.0 %collective-permute-done.7.u3 = bf16[8,64,1024]{2,1,0:T(8,128)(2,1)S(1)} collective-permute-done((bf16[8,64,1024]{2,1,0:T(8,128)(2,1)}, bf16[8,64,1024]{2,1,0:T(8,128)(2,1)S(1)}, u32[]{:S(2)}, u32[]{:S(2)}) %collective-permute-start.7) | collective-permute-done | bytes 1048608 | tf_op jit(solution)/shard_map/ppermute | solution.py:700
  29.2 2.8 %collective-permute-start.9 = (bf16[4,64,1024]{2,1,0:T(8,128)(2,1)}, bf16[4,64,1024]{2,1,0:T(8,128)(2,1)S(1)}, u32[]{:S(2)}, u32[]{:S(2)}) collective-permute-start(bf16[4,64,1024]{2,1,0:T(8,128)(2,1)} %slice.17), channel_id=1, source_target_pairs={{0,96},{32,0},{64,32},{96,64},{1,97},{33,1},{65,33},{97,65},{2,98}... | collective-permute-start | bytes 1572872 | tf_op jit(solution)/shard_map/ppermute | solution.py:700
  37.2 5.1 %collective-permute-done = s32[1,128]{1,0:T(1,128)S(1)} collective-permute-done((s32[1,128]{1,0:T(1,128)S(1)}, s32[1,128]{1,0:T(1,128)S(1)}, u32[]{:S(2)}, u32[]{:S(2)}) %collective-permute-start) | collective-permute-done | bytes 544 | tf_op jit(solution)/shard_map/ppermute | solution.py:700
  43.6 6.3 %zeta_home.1 = (bf16[18,64,128]{2,1,0:T(8,128)(2,1)S(1)}, bf16[18,64,128]{2,1,0:T(8,128)(2,1)S(1)}, bf16[18,64,128]{2,1,0:T(8,128)(2,1)S(1)}, bf16[18,64,128]{2,1,0:T(8,128)(2,1)S(1)}) custom-call(s32[4,128]{1,0:T(4,128)S(1)} %pad_add_fusion.req, bf16[8,64,1024]{2,1,0:T(8,128)(2,1)S(1)} %copy-done), custom_call_target="tpu_custom_call" | custom-call | tf_op jit(solution)/shard_map/zeta_home/pallas_call | solution.py:99
  49.9 3.7 %collective-permute-start.4 = (bf16[18,64,128]{2,1,0:T(8,128)(2,1)S(1)}, bf16[18,64,128]{2,1,0:T(8,128)(2,1)S(1)}, u32[]{:S(2)}, u32[]{:S(2)}) collective-permute-start(bf16[18,64,128]{2,1,0:T(8,128)(2,1)S(1)} %get-tuple-element.40), channel_id=1, source_target_pairs={{0,96},{32,0},{64,32},{96,64},{1,97},{33,1},{65,33},{97,65},{2,98}... | collective-permute-start | bytes 884744 | tf_op jit(solution)/shard_map/ppermute | solution.py:700
  55.1 6.9 %pairs_0.1 = (f32[8,64,1024]{2,1,0:T(8,128)S(1)}, bf16[32,64,64]{2,1,0:T(8,128)(2,1)S(1)}, bf16[4,64,1024]{2,1,0:T(8,128)(2,1)S(1)}) custom-call(s32[128]{0:T(128)S(1)} %concatenate.16.meta, bf16[8,64,1024]{2,1,0:T(8,128)(2,1)} %u0.1, bf16[18,64,128]{2,1,0:T(8,128)(2,1)S(1)} %get-tuple-element.42.z0, bf16[32,64,1024]{2,1,0:T(8,128)(2,1)} %lv.5, ...), custom_call_target="tpu_custom_call" | custom-call | tf_op jit(solution)/shard_map/pairs_0/pallas_call | solution.py:361
  62.1 4.4 %shard_map.122 = (bf16[32,64,64]{2,1,0:T(8,128)(2,1)S(1)}, bf16[4,64,1024]{2,1,0:T(8,128)(2,1)S(1)}) custom-call(s32[128]{0:T(128)S(1)} %concatenate.16.meta, bf16[8,64,1024]{2,1,0:T(8,128)(2,1)} %copy-done.3, bf16[8,64,1024]{2,1,0:T(8,128)(2,1)} %copy-done.2, bf16[32,64,64]{2,1,0:T(8,128)(2,1)S(1)} %get-tuple-element.44.mix_in, ...), custom_call_target="tpu_custom_call" | custom-call | tf_op jit(solution)/shard_map/pallas_call | solution.py:373
  67.4 5.2 %sum_a.1.acc_in = f32[8,64,1024]{2,1,0:T(8,128)S(1)} custom-call(s32[128]{0:T(128)S(1)} %concatenate.16.meta, bf16[18,64,128]{2,1,0:T(8,128)(2,1)S(1)} %collective-permute-done.4.z1, bf16[18,64,128]{2,1,0:T(8,128)(2,1)S(1)} %collective-permute-done.5.z3, f32[8,64,1024]{2,1,0:T(8,128)S(1)} %get-tuple-element.43.acc_in, ...), custom_call_target="tpu_custom_call" | custom-call | tf_op jit(solution)/shard_map/sum_a/pallas_call | solution.py:384
  74.2 5.6 %shard_map.123 = (bf16[32,64,64]{2,1,0:T(8,128)(2,1)S(1)}, bf16[4,64,1024]{2,1,0:T(8,128)(2,1)S(1)}) custom-call(s32[128]{0:T(128)S(1)} %concatenate.16.meta, bf16[4,64,1024]{2,1,0:T(8,128)(2,1)} %copy-done.6, bf16[4,64,1024]{2,1,0:T(8,128)(2,1)} %copy-done.7, bf16[32,64,64]{2,1,0:T(8,128)(2,1)S(1)} %get-tuple-element.46.mix.mix_in, ...), custom_call_target="tpu_custom_call" | custom-call | tf_op jit(solution)/shard_map/pallas_call | solution.py:373
  79.9 3.9 %sum_b.1 = (f32[4,64,1024]{2,1,0:T(8,128)S(1)}, f32[4,64,1024]{2,1,0:T(8,128)S(1)}) custom-call(s32[128]{0:T(128)S(1)} %concatenate.16.meta, bf16[18,64,128]{2,1,0:T(8,128)(2,1)S(1)} %collective-permute-done.3.z2, f32[8,64,1024]{2,1,0:T(8,128)S(1)} %sum_a.1.acc_in, bf16[32,64,64]{2,1,0:T(8,128)(2,1)S(1)} %get-tuple-element.48.mix, ...), custom_call_target="tpu_custom_call" | custom-call | tf_op jit(solution)/shard_map/sum_b/pallas_call | solution.py:396
  84.0 3.2 %collective-permute-start.24 = (bf16[8,64,1024]{2,1,0:T(8,128)(2,1)S(1)}, bf16[8,64,1024]{2,1,0:T(8,128)(2,1)S(1)}, u32[]{:S(2)}, u32[]{:S(2)}) collective-permute-start(bf16[8,64,1024]{2,1,0:T(8,128)(2,1)S(1)} %copy-done.1), channel_id=1, source_target_pairs={{0,96},{32,0},{64,32},{96,64},{1,97},{33,1},{65,33},{97,65},{2,98}... | collective-permute-start | bytes 3145736 | tf_op jit(solution)/shard_map/ppermute | solution.py:700
  87.9 4.4 %collective-permute-start.12 = (bf16[64,1024]{1,0:T(8,128)(2,1)S(1)}, bf16[64,1024]{1,0:T(8,128)(2,1)S(1)}, u32[]{:S(2)}, u32[]{:S(2)}) collective-permute-start(bf16[64,1024]{1,0:T(8,128)(2,1)S(1)} %bitcast.13), channel_id=1, source_target_pairs={{0,16},{1,17},{2,18},{3,19},{4,20},{5,21},{6,22},{7,23},{8,24},{9,... | collective-permute-start | bytes 393224 | tf_op jit(solution)/shard_map/ppermute | solution.py:710
  94.4 4.0 %collective-permute-done.12.c = bf16[64,1024]{1,0:T(8,128)(2,1)S(1)} collective-permute-done((bf16[64,1024]{1,0:T(8,128)(2,1)S(1)}, bf16[64,1024]{1,0:T(8,128)(2,1)S(1)}, u32[]{:S(2)}, u32[]{:S(2)}) %collective-permute-start.12) | collective-permute-done | bytes 131104 | tf_op jit(solution)/shard_map/ppermute | solution.py:710
  98.4 2.5 %collective-permute-start.14 = (bf16[64,1024]{1,0:T(8,128)(2,1)S(1)}, bf16[64,1024]{1,0:T(8,128)(2,1)S(1)}, u32[]{:S(2)}, u32[]{:S(2)}) collective-permute-start(bf16[64,1024]{1,0:T(8,128)(2,1)S(1)} %shard_map.124.a), channel_id=1, source_target_pairs={{0,2},{1,3},{2,4},{3,5},{4,6},{5,7},{6,0},{7,1},{8,10},{9,11},{10,... | collective-permute-start | bytes 393224 | tf_op jit(solution)/shard_map/ppermute | solution.py:710
  100.9 2.8 %collective-permute-start.15 = (bf16[64,1024]{1,0:T(8,128)(2,1)S(1)}, bf16[64,1024]{1,0:T(8,128)(2,1)S(1)}, u32[]{:S(2)}, u32[]{:S(2)}) collective-permute-start(bf16[64,1024]{1,0:T(8,128)(2,1)S(1)} %shard_map.124.a), channel_id=1, source_target_pairs={{0,4},{1,5},{2,6},{3,7},{4,0},{5,1},{6,2},{7,3},{8,12},{9,13},{10,... | collective-permute-start | bytes 393224 | tf_op jit(solution)/shard_map/ppermute | solution.py:710
  103.7 1.7 collective-permute-start.16
  105.4 5.3 %collective-permute-done.25.v3 = bf16[8,64,1024]{2,1,0:T(8,128)(2,1)S(1)} collective-permute-done((bf16[8,64,1024]{2,1,0:T(8,128)(2,1)S(1)}, bf16[8,64,1024]{2,1,0:T(8,128)(2,1)S(1)}, u32[]{:S(2)}, u32[]{:S(2)}) %collective-permute-start.25) | collective-permute-done | bytes 1048608 | tf_op jit(solution)/shard_map/ppermute | solution.py:700
  110.9 3.3 %collective-permute-start.27 = (bf16[4,64,1024]{2,1,0:T(8,128)(2,1)S(1)}, bf16[4,64,1024]{2,1,0:T(8,128)(2,1)S(1)}, u32[]{:S(2)}, u32[]{:S(2)}) collective-permute-start(bf16[4,64,1024]{2,1,0:T(8,128)(2,1)S(1)} %slice.19), channel_id=1, source_target_pairs={{0,96},{32,0},{64,32},{96,64},{1,97},{33,1},{65,33},{97,65},{2,98}... | collective-permute-start | bytes 1572872 | tf_op jit(solution)/shard_map/ppermute | solution.py:700
  114.2 3.0 %collective-permute-start.17 = (bf16[64,1024]{1,0:T(8,128)(2,1)S(1)}, bf16[64,1024]{1,0:T(8,128)(2,1)S(1)}, u32[]{:S(2)}, u32[]{:S(2)}) collective-permute-start(bf16[64,1024]{1,0:T(8,128)(2,1)S(1)} %shard_map.125.s0), channel_id=1, source_target_pairs={{0,24},{1,25},{2,26},{3,27},{4,28},{5,29},{6,30},{7,31},{8,0},{9,1... | collective-permute-start | bytes 393224 | tf_op jit(solution)/shard_map/ppermute | solution.py:710
  118.9 3.1 %collective-permute-done.17.s1 = bf16[64,1024]{1,0:T(8,128)(2,1)S(1)} collective-permute-done((bf16[64,1024]{1,0:T(8,128)(2,1)S(1)}, bf16[64,1024]{1,0:T(8,128)(2,1)S(1)}, u32[]{:S(2)}, u32[]{:S(2)}) %collective-permute-start.17) | collective-permute-done | bytes 131104 | tf_op jit(solution)/shard_map/ppermute | solution.py:710
  122.0 2.3 %collective-permute-done.18.s2 = bf16[64,1024]{1,0:T(8,128)(2,1)S(1)} collective-permute-done((bf16[64,1024]{1,0:T(8,128)(2,1)S(1)}, bf16[64,1024]{1,0:T(8,128)(2,1)S(1)}, u32[]{:S(2)}, u32[]{:S(2)}) %collective-permute-start.18) | collective-permute-done | bytes 131104 | tf_op jit(solution)/shard_map/ppermute | solution.py:710
  126.2 2.0 %make_plan.1.plan = s32[128]{0:T(128)S(1)} custom-call(s32[128]{0:T(128)S(1)} %concatenate.16.meta), custom_call_target="tpu_custom_call" | custom-call | tf_op jit(solution)/shard_map/make_plan/pallas_call | solution.py:171
  128.2 7.5 %proj_part.1 = (bf16[14,128,256]{2,1,0:T(8,128)(2,1)S(1)}, bf16[4,128,64]{2,1,0:T(8,128)(2,1)S(1)}, bf16[8,64,1024]{2,1,0:T(8,128)(2,1)S(1)}) custom-call(s32[128]{0:T(128)S(1)} %concatenate.16.meta, s32[128]{0:T(128)S(1)} %make_plan.1.plan, bf16[64,1024]{1,0:T(8,128)(2,1)S(1)} %shard_map.125.s0, bf16[64,1024]{1,0:T(8,128)(2,1)S(1)} %collective-permute-done.17.s1, ...), custom_call_target="tpu_custom_call" | custom-call | tf_op jit(solution)/shard_map/proj_part/pallas_call | solution.py:516
  136.8 5.4 %image_part.1 = (f32[16,32,512]{2,1,0:T(8,128)S(1)}, f32[16,32,512]{2,1,0:T(8,128)S(1)}) custom-call(s32[128]{0:T(128)S(1)} %concatenate.16.meta, s32[128]{0:T(128)S(1)} %make_plan.1.plan, bf16[14,128,256]{2,1,0:T(8,128)(2,1)S(1)} %get-tuple-element.62.p_ref, bf16[4,128,64]{2,1,0:T(8,128)(2,1)S(1)} %get-tuple-element.63.pn_ref, bf16[8,64,1024]{2,1,0:T(8,128)(2,1)} %v0.1, ...), custom_call_target="tpu_custom_call" | custom-call | tf_op jit(solution)/shard_map/image_part/pallas_call | solution.py:533
  142.5 2.5 %collective-permute-done.28.b = f32[16,32,512]{2,1,0:T(8,128)S(1)} collective-permute-done((f32[16,32,512]{2,1,0:T(8,128)S(1)}, f32[16,32,512]{2,1,0:T(8,128)S(1)}, u32[]{:S(2)}, u32[]{:S(2)}) %collective-permute-start.28) | collective-permute-done | bytes 1048608 | tf_op jit(solution)/shard_map/ppermute | solution.py:710
  145.7 2.4 %collective-permute-start.30 = (bf16[4,32,512]{2,1,0:T(8,128)(2,1)S(1)}, bf16[4,32,512]{2,1,0:T(8,128)(2,1)S(1)}, u32[]{:S(2)}, u32[]{:S(2)}) collective-permute-start(bf16[4,32,512]{2,1,0:T(8,128)(2,1)S(1)} %get-tuple-element.68), channel_id=1, source_target_pairs={{0,16},{1,17},{2,18},{3,19},{4,20},{5,21},{6,22},{7,23},{8,24},{9,... | collective-permute-start | bytes 393224 | tf_op jit(solution)/shard_map/ppermute | solution.py:710
  149.2 6.1 %collective-permute-done.29.b = bf16[4,32,512]{2,1,0:T(8,128)(2,1)S(1)} collective-permute-done((bf16[4,32,512]{2,1,0:T(8,128)(2,1)S(1)}, bf16[4,32,512]{2,1,0:T(8,128)(2,1)S(1)}, u32[]{:S(2)}, u32[]{:S(2)}) %collective-permute-start.29) | collective-permute-done | bytes 131104 | tf_op jit(solution)/shard_map/ppermute | solution.py:710
  156.5 2.2 %collective-permute-start.32 = (f32[32,512]{1,0:T(8,128)S(1)}, f32[32,512]{1,0:T(8,128)S(1)}, u32[]{:S(2)}, u32[]{:S(2)}) collective-permute-start(f32[32,512]{1,0:T(8,128)S(1)} %get-tuple-element.71), channel_id=1, source_target_pairs={{0,2},{1,3},{2,4},{3,5},{4,6},{5,7},{6,0},{7,1},{8,10},{9,11},{10,... | collective-permute-start | bytes 196616 | tf_op jit(solution)/shard_map/ppermute | solution.py:710
  158.8 2.6 %collective-permute-start.33 = (f32[32,512]{1,0:T(8,128)S(1)}, f32[32,512]{1,0:T(8,128)S(1)}, u32[]{:S(2)}, u32[]{:S(2)}) collective-permute-start(f32[32,512]{1,0:T(8,128)S(1)} %get-tuple-element.72), channel_id=1, source_target_pairs={{0,4},{1,5},{2,6},{3,7},{4,0},{5,1},{6,2},{7,3},{8,12},{9,13},{10,... | collective-permute-start | bytes 196616 | tf_op jit(solution)/shard_map/ppermute | solution.py:710
  163.0 1.9 %factor_0.1 = (f32[8,64,128]{2,1,0:T(8,128)S(1)}, f32[8,32,64]{2,1,0:T(8,128)S(1)}) custom-call(s32[128]{0:T(128)S(1)} %concatenate.16.meta, bf16[8,64,1024]{2,1,0:T(8,128)(2,1)S(1)} %get-tuple-element.57.s_ref), custom_call_target="tpu_custom_call" | custom-call | tf_op jit(solution)/shard_map/factor_0/pallas_call | solution.py:608
  164.9 4.4 %factor_1.1.m_in = f32[8,64,128]{2,1,0:T(8,128)S(1)} custom-call(f32[8,64,128]{2,1,0:T(8,128)S(1)} %get-tuple-element.58.m_in), custom_call_target="tpu_custom_call" | custom-call | tf_op jit(solution)/shard_map/factor_1/pallas_call | solution.py:616
  169.3 3.0 %factor_2.1 = (f32[8,32,64]{2,1,0:T(8,128)}, f32[8,64,64]{2,1,0:T(8,128)S(1)}) custom-call(f32[8,64,128]{2,1,0:T(8,128)S(1)} %factor_1.1.m_in, f32[8,32,64]{2,1,0:T(8,128)S(1)} %get-tuple-element.59.cols), custom_call_target="tpu_custom_call" | custom-call | tf_op jit(solution)/shard_map/factor_2/pallas_call | solution.py:619
  (86 shorter events, 29.5 us)
Async XLA Ops:
  0.6 26.3 %collective-permute-start.7 = (bf16[8,64,1024]{2,1,0:T(8,128)(2,1)}, bf16[8,64,1024]{2,1,0:T(8,128)(2,1)S(1)}, u32[]{:S(2)}, u32[]{:S(2)}) collective-permute-start(bf16[8,64,1024]{2,1,0:T(8,128)(2,1)} %u0.1), channel_id=1, source_target_pairs={{0,32},{32,64},{64,96},{96,0},{1,33},{33,65},{65,97},{97,1},{2,34}... | collective-permute-start | bytes 3145736 | tf_op jit(solution)/shard_map/ppermute | solution.py:700
  2.3 26.0 %collective-permute-start.6 = (bf16[8,64,1024]{2,1,0:T(8,128)(2,1)}, bf16[8,64,1024]{2,1,0:T(8,128)(2,1)S(1)}, u32[]{:S(2)}, u32[]{:S(2)}) collective-permute-start(bf16[8,64,1024]{2,1,0:T(8,128)(2,1)} %u0.1), channel_id=1, source_target_pairs={{0,96},{32,0},{64,32},{96,64},{1,97},{33,1},{65,33},{97,65},{2,98}... | collective-permute-start | bytes 3145736 | tf_op jit(solution)/shard_map/ppermute | solution.py:700
  27.9 44.8 %collective-permute-start.8 = (bf16[4,64,1024]{2,1,0:T(8,128)(2,1)}, bf16[4,64,1024]{2,1,0:T(8,128)(2,1)S(1)}, u32[]{:S(2)}, u32[]{:S(2)}) collective-permute-start(bf16[4,64,1024]{2,1,0:T(8,128)(2,1)} %slice.16), channel_id=1, source_target_pairs={{0,32},{32,64},{64,96},{96,0},{1,33},{33,65},{65,97},{97,1},{2,34}... | collective-permute-start | bytes 1572872 | tf_op jit(solution)/shard_map/ppermute | solution.py:700
  29.2 43.4 %collective-permute-start.9 = (bf16[4,64,1024]{2,1,0:T(8,128)(2,1)}, bf16[4,64,1024]{2,1,0:T(8,128)(2,1)S(1)}, u32[]{:S(2)}, u32[]{:S(2)}) collective-permute-start(bf16[4,64,1024]{2,1,0:T(8,128)(2,1)} %slice.17), channel_id=1, source_target_pairs={{0,96},{32,0},{64,32},{96,64},{1,97},{33,1},{65,33},{97,65},{2,98}... | collective-permute-start | bytes 1572872 | tf_op jit(solution)/shard_map/ppermute | solution.py:700
  32.8 9.5 %collective-permute-start = (s32[1,128]{1,0:T(1,128)S(1)}, s32[1,128]{1,0:T(1,128)S(1)}, u32[]{:S(2)}, u32[]{:S(2)}) collective-permute-start(s32[1,128]{1,0:T(1,128)S(1)} %bitcast.16), channel_id=1, source_target_pairs={{0,96},{32,0},{64,32},{96,64},{1,97},{33,1},{65,33},{97,65},{2,98}... | collective-permute-start | bytes 1544 | tf_op jit(solution)/shard_map/ppermute | solution.py:700
  33.3 9.0 %collective-permute-start.1 = (s32[1,128]{1,0:T(1,128)S(1)}, s32[1,128]{1,0:T(1,128)S(1)}, u32[]{:S(2)}, u32[]{:S(2)}) collective-permute-start(s32[1,128]{1,0:T(1,128)S(1)} %bitcast.17), channel_id=1, source_target_pairs={{0,64},{32,96},{64,0},{96,32},{1,65},{33,97},{65,1},{97,33},{2,66}... | collective-permute-start | bytes 1544 | tf_op jit(solution)/shard_map/ppermute | solution.py:700
  34.1 8.2 %collective-permute-start.2 = (s32[1,128]{1,0:T(1,128)S(1)}, s32[1,128]{1,0:T(1,128)S(1)}, u32[]{:S(2)}, u32[]{:S(2)}) collective-permute-start(s32[1,128]{1,0:T(1,128)S(1)} %bitcast.18), channel_id=1, source_target_pairs={{0,32},{32,64},{64,96},{96,0},{1,33},{33,65},{65,97},{97,1},{2,34}... | collective-permute-start | bytes 1544 | tf_op jit(solution)/shard_map/ppermute | solution.py:700
  49.9 16.6 %collective-permute-start.4 = (bf16[18,64,128]{2,1,0:T(8,128)(2,1)S(1)}, bf16[18,64,128]{2,1,0:T(8,128)(2,1)S(1)}, u32[]{:S(2)}, u32[]{:S(2)}) collective-permute-start(bf16[18,64,128]{2,1,0:T(8,128)(2,1)S(1)} %get-tuple-element.40), channel_id=1, source_target_pairs={{0,96},{32,0},{64,32},{96,64},{1,97},{33,1},{65,33},{97,65},{2,98}... | collective-permute-start | bytes 884744 | tf_op jit(solution)/shard_map/ppermute | solution.py:700
  53.6 13.8 %collective-permute-start.5 = (bf16[18,64,128]{2,1,0:T(8,128)(2,1)S(1)}, bf16[18,64,128]{2,1,0:T(8,128)(2,1)S(1)}, u32[]{:S(2)}, u32[]{:S(2)}) collective-permute-start(bf16[18,64,128]{2,1,0:T(8,128)(2,1)S(1)} %get-tuple-element.41), channel_id=1, source_target_pairs={{0,32},{32,64},{64,96},{96,0},{1,33},{33,65},{65,97},{97,1},{2,34}... | collective-permute-start | bytes 884744 | tf_op jit(solution)/shard_map/ppermute | solution.py:700
  53.6 26.2 %collective-permute-start.3 = (bf16[18,64,128]{2,1,0:T(8,128)(2,1)S(1)}, bf16[18,64,128]{2,1,0:T(8,128)(2,1)S(1)}, u32[]{:S(2)}, u32[]{:S(2)}) collective-permute-start(bf16[18,64,128]{2,1,0:T(8,128)(2,1)S(1)} %get-tuple-element.39), channel_id=1, source_target_pairs={{0,64},{32,96},{64,0},{96,32},{1,65},{33,97},{65,1},{97,33},{2,66}... | collective-permute-start | bytes 884744 | tf_op jit(solution)/shard_map/ppermute | solution.py:700
  83.8 3.4 %collective-permute-start.10 = (f32[4,64,1024]{2,1,0:T(8,128)S(1)}, f32[4,64,1024]{2,1,0:T(8,128)S(1)}, u32[]{:S(2)}, u32[]{:S(2)}) collective-permute-start(f32[4,64,1024]{2,1,0:T(8,128)S(1)} %get-tuple-element.52), channel_id=1, source_target_pairs={{0,1},{1,0},{2,3},{3,2},{4,5},{5,4},{6,7},{7,6},{8,9},{9,8},{10,11... | collective-permute-start | bytes 3145736 | tf_op jit(solution)/shard_map/ppermute | solution.py:710
  83.9 26.8 %collective-permute-start.25 = (bf16[8,64,1024]{2,1,0:T(8,128)(2,1)S(1)}, bf16[8,64,1024]{2,1,0:T(8,128)(2,1)S(1)}, u32[]{:S(2)}, u32[]{:S(2)}) collective-permute-start(bf16[8,64,1024]{2,1,0:T(8,128)(2,1)S(1)} %copy-done.1), channel_id=1, source_target_pairs={{0,32},{32,64},{64,96},{96,0},{1,33},{33,65},{65,97},{97,1},{2,34}... | collective-permute-start | bytes 3145736 | tf_op jit(solution)/shard_map/ppermute | solution.py:700
  84.0 26.8 %collective-permute-start.24 = (bf16[8,64,1024]{2,1,0:T(8,128)(2,1)S(1)}, bf16[8,64,1024]{2,1,0:T(8,128)(2,1)S(1)}, u32[]{:S(2)}, u32[]{:S(2)}) collective-permute-start(bf16[8,64,1024]{2,1,0:T(8,128)(2,1)S(1)} %copy-done.1), channel_id=1, source_target_pairs={{0,96},{32,0},{64,32},{96,64},{1,97},{33,1},{65,33},{97,65},{2,98}... | collective-permute-start | bytes 3145736 | tf_op jit(solution)/shard_map/ppermute | solution.py:700
  87.9 6.5 %collective-permute-start.11 = (bf16[64,1024]{1,0:T(8,128)(2,1)S(1)}, bf16[64,1024]{1,0:T(8,128)(2,1)S(1)}, u32[]{:S(2)}, u32[]{:S(2)}) collective-permute-start(bf16[64,1024]{1,0:T(8,128)(2,1)S(1)} %bitcast.14), channel_id=1, source_target_pairs={{0,8},{1,9},{2,10},{3,11},{4,12},{5,13},{6,14},{7,15},{8,16},{9,17... | collective-permute-start | bytes 393224 | tf_op jit(solution)/shard_map/ppermute | solution.py:710
  87.9 10.4 %collective-permute-start.12 = (bf16[64,1024]{1,0:T(8,128)(2,1)S(1)}, bf16[64,1024]{1,0:T(8,128)(2,1)S(1)}, u32[]{:S(2)}, u32[]{:S(2)}) collective-permute-start(bf16[64,1024]{1,0:T(8,128)(2,1)S(1)} %bitcast.13), channel_id=1, source_target_pairs={{0,16},{1,17},{2,18},{3,19},{4,20},{5,21},{6,22},{7,23},{8,24},{9,... | collective-permute-start | bytes 393224 | tf_op jit(solution)/shard_map/ppermute | solution.py:710
  92.3 6.0 %collective-permute-start.13 = (bf16[64,1024]{1,0:T(8,128)(2,1)S(1)}, bf16[64,1024]{1,0:T(8,128)(2,1)S(1)}, u32[]{:S(2)}, u32[]{:S(2)}) collective-permute-start(bf16[64,1024]{1,0:T(8,128)(2,1)S(1)} %bitcast.12), channel_id=1, source_target_pairs={{0,24},{1,25},{2,26},{3,27},{4,28},{5,29},{6,30},{7,31},{8,0},{9,1... | collective-permute-start | bytes 393224 | tf_op jit(solution)/shard_map/ppermute | solution.py:710
  98.4 15.7 %collective-permute-start.14 = (bf16[64,1024]{1,0:T(8,128)(2,1)S(1)}, bf16[64,1024]{1,0:T(8,128)(2,1)S(1)}, u32[]{:S(2)}, u32[]{:S(2)}) collective-permute-start(bf16[64,1024]{1,0:T(8,128)(2,1)S(1)} %shard_map.124.a), channel_id=1, source_target_pairs={{0,2},{1,3},{2,4},{3,5},{4,6},{5,7},{6,0},{7,1},{8,10},{9,11},{10,... | collective-permute-start | bytes 393224 | tf_op jit(solution)/shard_map/ppermute | solution.py:710
  100.9 13.2 %collective-permute-start.15 = (bf16[64,1024]{1,0:T(8,128)(2,1)S(1)}, bf16[64,1024]{1,0:T(8,128)(2,1)S(1)}, u32[]{:S(2)}, u32[]{:S(2)}) collective-permute-start(bf16[64,1024]{1,0:T(8,128)(2,1)S(1)} %shard_map.124.a), channel_id=1, source_target_pairs={{0,4},{1,5},{2,6},{3,7},{4,0},{5,1},{6,2},{7,3},{8,12},{9,13},{10,... | collective-permute-start | bytes 393224 | tf_op jit(solution)/shard_map/ppermute | solution.py:710
  103.7 10.4 %collective-permute-start.16 = (bf16[64,1024]{1,0:T(8,128)(2,1)S(1)}, bf16[64,1024]{1,0:T(8,128)(2,1)S(1)}, u32[]{:S(2)}, u32[]{:S(2)}) collective-permute-start(bf16[64,1024]{1,0:T(8,128)(2,1)S(1)} %shard_map.124.a), channel_id=1, source_target_pairs={{0,6},{1,7},{2,0},{3,1},{4,2},{5,3},{6,4},{7,5},{8,14},{9,15},{10,... | collective-permute-start | bytes 393224 | tf_op jit(solution)/shard_map/ppermute | solution.py:710
  110.7 25.1 %collective-permute-start.26 = (bf16[4,64,1024]{2,1,0:T(8,128)(2,1)S(1)}, bf16[4,64,1024]{2,1,0:T(8,128)(2,1)S(1)}, u32[]{:S(2)}, u32[]{:S(2)}) collective-permute-start(bf16[4,64,1024]{2,1,0:T(8,128)(2,1)S(1)} %slice.18), channel_id=1, source_target_pairs={{0,32},{32,64},{64,96},{96,0},{1,33},{33,65},{65,97},{97,1},{2,34}... | collective-permute-start | bytes 1572872 | tf_op jit(solution)/shard_map/ppermute | solution.py:700
  110.9 24.9 %collective-permute-start.27 = (bf16[4,64,1024]{2,1,0:T(8,128)(2,1)S(1)}, bf16[4,64,1024]{2,1,0:T(8,128)(2,1)S(1)}, u32[]{:S(2)}, u32[]{:S(2)}) collective-permute-start(bf16[4,64,1024]{2,1,0:T(8,128)(2,1)S(1)} %slice.19), channel_id=1, source_target_pairs={{0,96},{32,0},{64,32},{96,64},{1,97},{33,1},{65,33},{97,65},{2,98}... | collective-permute-start | bytes 1572872 | tf_op jit(solution)/shard_map/ppermute | solution.py:700
  114.2 7.8 %collective-permute-start.17 = (bf16[64,1024]{1,0:T(8,128)(2,1)S(1)}, bf16[64,1024]{1,0:T(8,128)(2,1)S(1)}, u32[]{:S(2)}, u32[]{:S(2)}) collective-permute-start(bf16[64,1024]{1,0:T(8,128)(2,1)S(1)} %shard_map.125.s0), channel_id=1, source_target_pairs={{0,24},{1,25},{2,26},{3,27},{4,28},{5,29},{6,30},{7,31},{8,0},{9,1... | collective-permute-start | bytes 393224 | tf_op jit(solution)/shard_map/ppermute | solution.py:710
  117.2 7.0 %collective-permute-start.18 = (bf16[64,1024]{1,0:T(8,128)(2,1)S(1)}, bf16[64,1024]{1,0:T(8,128)(2,1)S(1)}, u32[]{:S(2)}, u32[]{:S(2)}) collective-permute-start(bf16[64,1024]{1,0:T(8,128)(2,1)S(1)} %shard_map.125.s0), channel_id=1, source_target_pairs={{0,16},{1,17},{2,18},{3,19},{4,20},{5,21},{6,22},{7,23},{8,24},{9,... | collective-permute-start | bytes 393224 | tf_op jit(solution)/shard_map/ppermute | solution.py:710
  117.6 8.1 %collective-permute-start.19 = (bf16[64,1024]{1,0:T(8,128)(2,1)S(1)}, bf16[64,1024]{1,0:T(8,128)(2,1)S(1)}, u32[]{:S(2)}, u32[]{:S(2)}) collective-permute-start(bf16[64,1024]{1,0:T(8,128)(2,1)S(1)} %shard_map.125.s0), channel_id=1, source_target_pairs={{0,8},{1,9},{2,10},{3,11},{4,12},{5,13},{6,14},{7,15},{8,16},{9,17... | collective-permute-start | bytes 393224 | tf_op jit(solution)/shard_map/ppermute | solution.py:710
  122.0 3.7 %collective-permute-start.20 = (bf16[64,1024]{1,0:T(8,128)(2,1)S(1)}, bf16[64,1024]{1,0:T(8,128)(2,1)S(1)}, u32[]{:S(2)}, u32[]{:S(2)}) collective-permute-start(bf16[64,1024]{1,0:T(8,128)(2,1)S(1)} %shard_map.125.s0), channel_id=1, source_target_pairs={{0,1},{1,0},{2,3},{3,2},{4,5},{5,4},{6,7},{7,6},{8,9},{9,8},{10,11... | collective-permute-start | bytes 393224 | tf_op jit(solution)/shard_map/ppermute | solution.py:710
  124.2 4.0 %collective-permute-start.21 = (bf16[64,1024]{1,0:T(8,128)(2,1)S(1)}, bf16[64,1024]{1,0:T(8,128)(2,1)S(1)}, u32[]{:S(2)}, u32[]{:S(2)}) collective-permute-start(bf16[64,1024]{1,0:T(8,128)(2,1)S(1)} %collective-permute-done.17.s1), channel_id=1, source_target_pairs={{0,1},{1,0},{2,3},{3,2},{4,5},{5,4},{6,7},{7,6},{8,9},{9,8},{10,11... | collective-permute-start | bytes 393224 | tf_op jit(solution)/shard_map/ppermute | solution.py:710
  145.6 9.7 %collective-permute-start.29 = (bf16[4,32,512]{2,1,0:T(8,128)(2,1)S(1)}, bf16[4,32,512]{2,1,0:T(8,128)(2,1)S(1)}, u32[]{:S(2)}, u32[]{:S(2)}) collective-permute-start(bf16[4,32,512]{2,1,0:T(8,128)(2,1)S(1)} %get-tuple-element.67), channel_id=1, source_target_pairs={{0,8},{1,9},{2,10},{3,11},{4,12},{5,13},{6,14},{7,15},{8,16},{9,17... | collective-permute-start | bytes 393224 | tf_op jit(solution)/shard_map/ppermute | solution.py:710
  145.7 9.6 %collective-permute-start.30 = (bf16[4,32,512]{2,1,0:T(8,128)(2,1)S(1)}, bf16[4,32,512]{2,1,0:T(8,128)(2,1)S(1)}, u32[]{:S(2)}, u32[]{:S(2)}) collective-permute-start(bf16[4,32,512]{2,1,0:T(8,128)(2,1)S(1)} %get-tuple-element.68), channel_id=1, source_target_pairs={{0,16},{1,17},{2,18},{3,19},{4,20},{5,21},{6,22},{7,23},{8,24},{9,... | collective-permute-start | bytes 393224 | tf_op jit(solution)/shard_map/ppermute | solution.py:710
  148.1 7.8 %collective-permute-start.31 = (bf16[4,32,512]{2,1,0:T(8,128)(2,1)S(1)}, bf16[4,32,512]{2,1,0:T(8,128)(2,1)S(1)}, u32[]{:S(2)}, u32[]{:S(2)}) collective-permute-start(bf16[4,32,512]{2,1,0:T(8,128)(2,1)S(1)} %get-tuple-element.69), channel_id=1, source_target_pairs={{0,24},{1,25},{2,26},{3,27},{4,28},{5,29},{6,30},{7,31},{8,0},{9,1... | collective-permute-start | bytes 393224 | tf_op jit(solution)/shard_map/ppermute | solution.py:710
  156.5 15.8 %collective-permute-start.32 = (f32[32,512]{1,0:T(8,128)S(1)}, f32[32,512]{1,0:T(8,128)S(1)}, u32[]{:S(2)}, u32[]{:S(2)}) collective-permute-start(f32[32,512]{1,0:T(8,128)S(1)} %get-tuple-element.71), channel_id=1, source_target_pairs={{0,2},{1,3},{2,4},{3,5},{4,6},{5,7},{6,0},{7,1},{8,10},{9,11},{10,... | collective-permute-start | bytes 196616 | tf_op jit(solution)/shard_map/ppermute | solution.py:710
  158.8 13.6 %collective-permute-start.33 = (f32[32,512]{1,0:T(8,128)S(1)}, f32[32,512]{1,0:T(8,128)S(1)}, u32[]{:S(2)}, u32[]{:S(2)}) collective-permute-start(f32[32,512]{1,0:T(8,128)S(1)} %get-tuple-element.72), channel_id=1, source_target_pairs={{0,4},{1,5},{2,6},{3,7},{4,0},{5,1},{6,2},{7,3},{8,12},{9,13},{10,... | collective-permute-start | bytes 196616 | tf_op jit(solution)/shard_map/ppermute | solution.py:710
  161.4 11.0 %collective-permute-start.34 = (f32[32,512]{1,0:T(8,128)S(1)}, f32[32,512]{1,0:T(8,128)S(1)}, u32[]{:S(2)}, u32[]{:S(2)}) collective-permute-start(f32[32,512]{1,0:T(8,128)S(1)} %get-tuple-element.73), channel_id=1, source_target_pairs={{0,6},{1,7},{2,0},{3,1},{4,2},{5,3},{6,4},{7,5},{8,14},{9,15},{10,... | collective-permute-start | bytes 196616 | tf_op jit(solution)/shard_map/ppermute | solution.py:710
  (13 other events, 135.5 us)
